TPU v7x, 512 devices: a whole 4x4x16 slice. The times are simulated.
512 devices in a mesh: mesh: 32 (over z, core), samp: 16 (over y, x).
Axes of the slice: x: 4, y: 4, z: 16, core: 2. Of those that a mesh axis runs over, the one named last changes fastest.
Arguments:
- resid_in: float32 [1024, 98304], P('samp', 'mesh'), may hold values from -10 to 10
- recycle_u: bfloat16 [64, 98304], P('samp', 'mesh'), may hold values from -0.75 to 0.75
- recycle_c: bfloat16 [64, 98304], P('samp', 'mesh'), may hold values from -0.01953125 to 0.01953125
- stiff: bfloat16 [512, 192, 1152], P('mesh'), may hold values from -0.1875 to 0.1875
- diag_scale: float32 [98304], P('mesh'), may hold values from 1 to 8
- pattern: int32 [512, 6], P('mesh'), may hold values from 0 to 31, as said below
- send_list: int32 [64, 8], P('mesh'), may hold values from 0 to 15, as said below
- part_sizes: int32 [32], P('mesh'), may hold values from 8 to 16, as said below
Outputs:
- solution: float32 [1024, 98304], P('samp', 'mesh')
- residual: float32 [1024, 98304], P('samp', 'mesh')
- recycle_coef: float32 [64, 1024], P(None, 'samp')
Inputs may be any that keep to these rules, and one draw needn't show every extreme that they name: `part_sizes`: one partition has 16 live blocks and one has 8. Entries of send_list for partition p are live local blocks of p (below part_sizes[p]); repeats may occur. `pattern`: slot 0 of each block row is its own block; entries below 16 name live local blocks, 16 to 23 left ghosts, the rest right ghosts.
All inputs are finite; a program needn't handle non-finite values.
Results may differ from a plain program's by a relative error of at most 0.0063.
Values may be sent and summed in bfloat16 or wider, within the bound.
A program may use at most 64 MiB of HBM per device.

v0:
```python
import jax
import jax.numpy as jnp
from jax import lax
from jax.sharding import PartitionSpec as P

ITERS = 2


highest = lax.Precision.HIGHEST


def passed_along(x, axis, by):
    size = lax.axis_size(axis)
    pairs = [(i, i + by) for i in range(size) if 0 <= i + by < size]
    return lax.ppermute(x, axis, pairs)


def slot_product(picks, stiff):
    load_cols = picks.shape[0]
    flat = picks.reshape(load_cols, stiff.shape[0], stiff.shape[2])
    return jnp.einsum("lik,ick->lic", flat, stiff, preferred_element_type=jnp.float32)


def neighbour_ghosts(to_right, to_left):
    left_ghost = passed_along(to_right, "mesh", 1)
    right_ghost = passed_along(to_left, "mesh", -1)
    return jnp.concatenate([left_ghost, right_ghost], 1)


def apply_stiff(rounded, stiff, diag_scale, pattern, send_list, alive_mask):
    load_cols = rounded.shape[0]
    block_rows = stiff.shape[0]
    block_dofs = stiff.shape[1]
    clusters = rounded.reshape(load_cols, block_rows, block_dofs)
    to_right = clusters[:, send_list[0]]
    to_left = clusters[:, send_list[1]]
    ghosts = neighbour_ghosts(to_right, to_left)
    extended = jnp.concatenate([clusters, ghosts], 1)
    coupled = slot_product(extended[:, pattern], stiff)
    coupled = coupled.reshape(load_cols, block_rows * block_dofs)
    return alive_mask * (diag_scale * rounded.astype(jnp.float32) + coupled)


def per_device(resid_in, recycle_u, recycle_c, stiff, diag_scale, pattern, send_list, part_sizes):
    block_rows = stiff.shape[0]
    block_dofs = stiff.shape[1]
    block_ids = jnp.arange(block_rows, dtype=jnp.int32)
    alive_blocks = (block_ids < part_sizes[0]).astype(jnp.float32)
    alive_mask = jnp.broadcast_to(alive_blocks[:, None], (block_rows, block_dofs)).reshape(
        block_rows * block_dofs
    )
    panel_u_half, panel_c_half = (
        lax.all_gather(recycle_u, "samp", axis=0, tiled=True),
        lax.all_gather(recycle_c, "samp", axis=0, tiled=True),
    )
    panel_c = panel_c_half.astype(jnp.float32)
    current = alive_mask * resid_in
    local_coef = jnp.dot(
        panel_c_half, current.astype(jnp.bfloat16).T, preferred_element_type=jnp.float32
    )
    recycle_coef = lax.psum(local_coef, "mesh")
    current = current - alive_mask * jnp.dot(recycle_coef.T, panel_c, precision=highest)
    carried = recycle_coef
    direct = jnp.zeros_like(current)
    for iteration in range(ITERS):
        rounded = current.astype(jnp.bfloat16)
        image_vec = apply_stiff(rounded, stiff, diag_scale, pattern, send_list, alive_mask)
        local_proj = jnp.dot(panel_c, image_vec.T, precision=highest)
        projected = lax.psum(local_proj, "mesh")
        image_vec = image_vec - alive_mask * jnp.dot(projected.T, panel_c, precision=highest)
        numerator, denominator = lax.psum(
            (jnp.sum(image_vec * current, axis=1), jnp.sum(image_vec * image_vec, axis=1)), "mesh"
        )
        step_size = numerator / denominator
        direct = direct + step_size[:, None] * rounded.astype(jnp.float32)
        carried = carried - projected * step_size[None, :]
        current = current - step_size[:, None] * image_vec
    solution = (
        alive_mask * jnp.dot(carried.T, panel_u_half.astype(jnp.float32), precision=highest)
        + direct
    )
    return (solution, current, recycle_coef)


def solution(mesh):
    return jax.shard_map(
        per_device,
        mesh=mesh,
        in_specs=(
            P("samp", "mesh"),
            P("samp", "mesh"),
            P("samp", "mesh"),
            P("mesh", None, None),
            P("mesh"),
            P("mesh", None),
            P("mesh", None),
            P("mesh"),
        ),
        out_specs=(P("samp", "mesh"), P("samp", "mesh"), P(None, "samp")),
        check_vma=False,
    )
```

profile of v0, /device:TPU:1, one launch (start us, length us, event | category | flops | bytes accessed | tf_op | source)
XLA Modules:
  0.0 503.5 jit_solution(13028145403141466484)
XLA Ops:
  1.3 0.1 broadcast_in_dim.4
  1.4 0.1 mul.52
  1.4 19.8 %all-gather = bf16[16,4,3072]{2,1,0:T(4,128)(2,1)S(1)} all-gather(bf16[1,4,3072]{2,1,0:T(4,128)(2,1)} %bitcast.55), channel_id=1, replica_groups=mesh['mesh'=32,'samp'=16] {'samp'}, dimensions={0}, use_global_device_ids=true | all-gather | bytes 417792 | tf_op jit(solution)/shard_map/all_gather | solution.py:54
  21.3 0.1 reshape.150
  21.4 0.0 copy-start.13
  21.4 1.4 convolution_bitcast_fusion.4
  22.8 99.0 %psum.49 = f32[64,64]{0,1:T(8,128)S(1)} all-reduce(f32[64,64]{0,1:T(8,128)S(1)} %convolution_bitcast_fusion.4), channel_id=1, replica_groups=mesh['mesh'=32,'samp'=16] {'mesh'}, use_global_device_ids=true, to_apply=%region_0.0 | all-reduce | flops 4096 | bytes 32768 | tf_op jit(solution)/shard_map/psum | solution.py:61
  121.8 1.7 fusion.25
  123.4 0.0 copy-start
  123.4 0.6 reshape.91
  124.0 0.2 copy.33
  124.2 0.0 copy-start.11
  124.3 0.6 gather_fusion
  124.8 3.6 collective-permute-start
  128.5 0.6 gather_fusion.1
  129.0 3.1 collective-permute-start.1
  132.2 0.0 copy-done.11
  132.2 0.0 copy-done.12
  132.2 0.1 copy.34
  132.3 0.1 reshape.115
  132.4 0.0 collective-permute-done
  132.4 0.0 copy-start.7
  132.4 0.7 copy-done.7
  133.1 3.7 collective-permute-done.1
  136.8 1.2 pad_maximum_fusion
  138.1 2.6 gather_fusion.2
  140.6 6.1 %copy.45 = bf16[64,16,6,192]{3,2,0,1:T(8,128)(2,1)} copy(bf16[64,16,6,192]{3,0,2,1:T(8,128)(2,1)} %bitcast.51) | data formatting | bytes 4718592 | tf_op jit(solution)/shard_map/reshape | solution.py:20
  146.8 6.8 %reshape.153 = bf16[64,16,1152]{2,0,1:T(8,128)(2,1)} reshape(bf16[64,16,6,192]{3,2,0,1:T(8,128)(2,1)} %copy.45) | data formatting | bytes 4718592 | tf_op jit(solution)/shard_map/reshape | solution.py:20
  153.6 6.3 %convolution_bitcast_fusion.1 = f32[64,16,192]{2,0,1:T(8,128)S(1)} fusion(bf16[64,16,1152]{2,0,1:T(8,128)(2,1)} %reshape.153, bf16[16,192,1152]{2,1,0:T(8,128)(2,1)} %param.11), kind=kOutput, calls=%fused_computation.15 | convolution fusion | flops 452984832 | bytes 10223616 | tf_op jit(solution)/shard_map/lik,ick->lic/dot_general | solution.py:21
  159.9 0.0 copy-start.8
  159.9 1.6 copy.37
  161.5 1.6 reshape.93
  163.1 0.6 convolution_bitcast_fusion.3
  163.7 87.0 %psum.50 = f32[64,64]{0,1:T(8,128)S(1)} all-reduce(f32[64,64]{0,1:T(8,128)S(1)} %convolution_bitcast_fusion.3), channel_id=1, replica_groups=mesh['mesh'=32,'samp'=16] {'mesh'}, use_global_device_ids=true, to_apply=%region_1.0 | all-reduce | flops 4096 | bytes 32768 | tf_op jit(solution)/shard_map/psum | solution.py:69
  250.6 1.6 multiply_reduce_fusion.2
  252.2 0.0 copy-start.10
  252.3 48.7 %all-reduce.1 = (f32[64]{0:T(128)S(1)}, f32[64]{0:T(128)S(1)}) all-reduce(f32[64]{0:T(128)S(1)} %get-tuple-element.15, f32[64]{0:T(128)S(1)} %get-tuple-element.14), channel_id=1, replica_groups=mesh['mesh'=32,'samp'=16] {'mesh'}, use_global_device_ids=true, to_apply=%region_3.0 | all-reduce | flops 128 | bytes 1024 | tf_op jit(solution)/shard_map/psum | solution.py:71
  301.0 1.5 fusion.24
  302.5 0.6 reshape.94
  303.1 0.2 copy.40
  303.3 1.4 gather_fusion.3
  304.7 0.7 gather_fusion.4
  305.4 1.9 collective-permute-start.2
  307.3 3.1 collective-permute-start.3
  310.4 0.7 copy.44
  311.1 18.6 %all-gather.1 = bf16[16,4,3072]{2,1,0:T(4,128)(2,1)S(1)} all-gather(bf16[1,4,3072]{2,1,0:T(4,128)(2,1)S(1)} %bitcast.56), channel_id=1, replica_groups=mesh['mesh'=32,'samp'=16] {'samp'}, dimensions={0}, use_global_device_ids=true | all-gather | bytes 417792 | tf_op jit(solution)/shard_map/all_gather | solution.py:53
  329.7 0.8 reshape.152
  330.6 0.0 collective-permute-done.2
  330.6 0.0 collective-permute-done.3
  330.6 1.2 pad_maximum_fusion.1
  331.8 2.6 gather_fusion.5
  334.4 6.1 %copy.46 = bf16[64,16,6,192]{3,2,0,1:T(8,128)(2,1)} copy(bf16[64,16,6,192]{3,0,2,1:T(8,128)(2,1)} %bitcast.50) | data formatting | bytes 4718592 | tf_op jit(solution)/shard_map/reshape | solution.py:20
  340.5 6.8 %reshape.154 = bf16[64,16,1152]{2,0,1:T(8,128)(2,1)} reshape(bf16[64,16,6,192]{3,2,0,1:T(8,128)(2,1)} %copy.46) | data formatting | bytes 4718592 | tf_op jit(solution)/shard_map/reshape | solution.py:20
  347.3 6.3 %convolution_bitcast_fusion = f32[64,16,192]{2,0,1:T(8,128)S(1)} fusion(bf16[64,16,1152]{2,0,1:T(8,128)(2,1)} %reshape.154, bf16[16,192,1152]{2,1,0:T(8,128)(2,1)} %param.11), kind=kOutput, calls=%fused_computation.14 | convolution fusion | flops 452984832 | bytes 10223616 | tf_op jit(solution)/shard_map/lik,ick->lic/dot_general | solution.py:21
  353.6 0.0 copy-start.9
  353.6 1.6 copy.43
  355.2 1.6 reshape.96
  356.9 0.6 convolution_bitcast_fusion.2
  357.4 0.0 copy-start.1
  357.5 94.2 %psum.53 = f32[64,64]{0,1:T(8,128)S(1)} all-reduce(f32[64,64]{0,1:T(8,128)S(1)} %convolution_bitcast_fusion.2), channel_id=1, replica_groups=mesh['mesh'=32,'samp'=16] {'mesh'}, use_global_device_ids=true, to_apply=%region_6.0 | all-reduce | flops 4096 | bytes 32768 | tf_op jit(solution)/shard_map/psum | solution.py:69
  451.7 1.6 multiply_reduce_fusion
  453.3 46.4 %all-reduce = (f32[64]{0:T(128)S(1)}, f32[64]{0:T(128)S(1)}) all-reduce(f32[64]{0:T(128)S(1)} %get-tuple-element.13, f32[64]{0:T(128)S(1)} %get-tuple-element.12), channel_id=1, replica_groups=mesh['mesh'=32,'samp'=16] {'mesh'}, use_global_device_ids=true, to_apply=%region_8.0 | all-reduce | flops 128 | bytes 1024 | tf_op jit(solution)/shard_map/psum | solution.py:71
  499.8 2.2 multiply_subtract_fusion
  502.0 1.5 fusion.3
  (30 shorter events, 0.1 us)
Async XLA Ops:
  21.3 102.9 %copy-start.16 = (s32[2,8]{1,0:T(2,128)S(1)}, s32[2,8]{1,0:T(2,128)}, u32[]{:S(2)}) copy-start(s32[2,8]{1,0:T(2,128)} %param.14) | copy-start | bytes 196
  21.4 110.8 %copy-start.13 = (s32[16,6]{0,1:T(8,128)S(1)}, s32[16,6]{0,1:T(8,128)}, u32[]{:S(2)}) copy-start(s32[16,6]{0,1:T(8,128)} %param.13) | copy-start | bytes 1156
  121.8 1.7 copy-start.2
  123.4 127.2 %copy-start = (f32[64,3072]{1,0:T(8,128)}, f32[64,3072]{1,0:T(8,128)S(1)}, u32[]{:S(2)}) copy-start(f32[64,3072]{1,0:T(8,128)S(1)} %get-tuple-element.25) | copy-start | bytes 2359300
  124.2 7.9 %copy-start.11 = (s32[1024]{0:T(1024)}, s32[1024]{0:T(1024)S(1)}, u32[]{:S(2)}) copy-start(s32[1024]{0:T(1024)S(1)} %get-tuple-element.28) | copy-start | bytes 12292
  124.3 7.9 %copy-start.12 = (s32[1024]{0:T(1024)}, s32[1024]{0:T(1024)S(1)}, u32[]{:S(2)}) copy-start(s32[1024]{0:T(1024)S(1)} %get-tuple-element.29) | copy-start | bytes 12292
  124.8 7.6 %collective-permute-start = (bf16[64,8,192]{2,0,1:T(8,128)(2,1)S(1)}, bf16[64,8,192]{2,0,1:T(8,128)(2,1)S(1)}, u32[]{:S(2)}, u32[]{:S(2)}) collective-permute-start(bf16[64,8,192]{2,0,1:T(8,128)(2,1)S(1)} %bitcast.52), channel_id=1, source_target_pairs={{0,16},{16,32},{32,48},{48,64},{64,80},{80,96},{96,112},{112,128},... | collective-permute-start | bytes 589832 | tf_op jit(solution)/shard_map/ppermute | solution.py:15
  129.0 7.8 %collective-permute-start.1 = (bf16[64,8,192]{2,0,1:T(8,128)(2,1)S(1)}, bf16[64,8,192]{2,0,1:T(8,128)(2,1)}, u32[]{:S(2)}, u32[]{:S(2)}) collective-permute-start(bf16[64,8,192]{2,0,1:T(8,128)(2,1)S(1)} %bitcast.54), channel_id=1, source_target_pairs={{16,0},{32,16},{48,32},{64,48},{80,64},{96,80},{112,96},{128,112},... | collective-permute-start | bytes 589832 | tf_op jit(solution)/shard_map/ppermute | solution.py:15
  132.4 0.7 copy-start.7
  159.9 3.2 copy-start.8
  250.6 52.5 %copy-start.5 = (f32[64,64]{0,1:T(8,128)}, f32[64,64]{0,1:T(8,128)S(1)}, u32[]{:S(2)}) copy-start(f32[64,64]{0,1:T(8,128)S(1)} %psum.50) | copy-start | bytes 49156
  252.2 58.2 %copy-start.3 = (f32[64,64]{0,1:T(8,128)S(1)}, f32[64,64]{0,1:T(8,128)}, u32[]{:S(2)}) copy-start(f32[64,64]{0,1:T(8,128)} %copy-done.2) | copy-start | bytes 49156
  252.2 58.9 %copy-start.10 = (bf16[4,3072]{1,0:T(4,128)(2,1)S(1)}, bf16[4,3072]{1,0:T(4,128)(2,1)}, u32[]{:S(2)}) copy-start(bf16[4,3072]{1,0:T(4,128)(2,1)} %param.9) | copy-start | bytes 73732
  300.9 29.6 %copy-start.14 = (f32[64]{0:T(128)}, f32[64]{0:T(128)S(1)}, u32[]{:S(2)}) copy-start(f32[64]{0:T(128)S(1)} %div.6) | copy-start | bytes 772
  305.4 25.2 %collective-permute-start.2 = (bf16[64,8,192]{2,0,1:T(8,128)(2,1)}, bf16[64,8,192]{2,0,1:T(8,128)(2,1)}, u32[]{:S(2)}, u32[]{:S(2)}) collective-permute-start(bf16[64,8,192]{2,0,1:T(8,128)(2,1)} %bitcast.13), channel_id=1, source_target_pairs={{0,16},{16,32},{32,48},{48,64},{64,80},{80,96},{96,112},{112,128},... | collective-permute-start | bytes 589832 | tf_op jit(solution)/shard_map/ppermute | solution.py:15
  307.3 23.3 %collective-permute-start.3 = (bf16[64,8,192]{2,0,1:T(8,128)(2,1)S(1)}, bf16[64,8,192]{2,0,1:T(8,128)(2,1)}, u32[]{:S(2)}, u32[]{:S(2)}) collective-permute-start(bf16[64,8,192]{2,0,1:T(8,128)(2,1)S(1)} %bitcast.53), channel_id=1, source_target_pairs={{16,0},{32,16},{48,32},{64,48},{80,64},{96,80},{112,96},{128,112},... | collective-permute-start | bytes 589832 | tf_op jit(solution)/shard_map/ppermute | solution.py:15
  353.6 3.2 copy-start.9
  357.4 144.5 %copy-start.1 = (bf16[64,3072]{1,0:T(8,128)(2,1)S(1)}, bf16[64,3072]{1,0:T(8,128)(2,1)}, u32[]{:S(2)}) copy-start(bf16[64,3072]{1,0:T(8,128)(2,1)} %reshape.152) | copy-start | bytes 1179652
  357.5 144.5 %copy-start.4 = (f32[64,64]{0,1:T(8,128)S(1)}, f32[64,64]{0,1:T(8,128)}, u32[]{:S(2)}) copy-start(f32[64,64]{0,1:T(8,128)} %copy-done.2) | copy-start | bytes 49156
  357.5 144.5 %copy-start.6 = (f32[64,64]{0,1:T(8,128)S(1)}, f32[64,64]{0,1:T(8,128)}, u32[]{:S(2)}) copy-start(f32[64,64]{0,1:T(8,128)} %copy-done.5) | copy-start | bytes 49156
  357.5 144.5 %copy-start.15 = (f32[64]{0:T(128)S(1)}, f32[64]{0:T(128)}, u32[]{:S(2)}) copy-start(f32[64]{0:T(128)} %copy-done.14) | copy-start | bytes 772
where the time goes:
time: 505 us; the launch traced here: 503 us
  blocking collectives  414 us (82%)
  local copies, waits for them, and re-layouts  44.8 us (9%)
  matrix products  21.5 us (4%)
  starting transfers between devices  11.8 us (2%)
  other arithmetic  6.2 us (1%)
    psum x2, blocking collectives, per_device(): projected = lax.psum(local_proj, 'mesh')  181 us
    psum x1, blocking collectives, per_device(): recycle_coef = lax.psum(local_coef, 'mesh')  99 us
    psum x2, blocking collectives, per_device(): lax.psum((jnp.sum(image_vec * current, axis=1), jnp.sum(image_vec * image...  95.1 us
    reshape x4, local copies, waits for them, and re-layouts, slot_product(): flat = picks.reshape(load_cols, stiff.shape[0], stiff.shape[2])  25.9 us
    all_gather x1, blocking collectives, per_device(): lax.all_gather(recycle_c, 'samp', axis=0, tiled=True)  19.8 us
    all_gather x1, blocking collectives, per_device(): lax.all_gather(recycle_u, 'samp', axis=0, tiled=True)  18.6 us
    dot_general x2, matrix products, slot_product(): jnp.einsum('lik,ick->lic', flat, stiff, preferred_element_type=jnp.float32)  12.6 us
    ppermute x4, starting transfers between devices, passed_along(): return lax.ppermute(x, axis, pairs)  11.8 us
  transfers between devices with their start and end apart: 4, of which 1 were waited for; matrix products, arithmetic and copies ran while one was open for 0% of the time, Pallas kernels for 0%

commit v1 on v0

v1 whole, which is shorter than its diff:
```python
import functools

import jax
import jax.numpy as jnp
from jax import lax
from jax.experimental import pallas as pl
from jax.experimental.pallas import tpu as pltpu
from jax.sharding import PartitionSpec as P

MESH = pl.DeviceIdType.MESH
F32 = jnp.float32
BF16 = jnp.bfloat16
LANES = 128
BLK = 192
PAIR = 2 * BLK
SLOTS = 6
GHOST = 8
ITERS = 2
TILES = 8


def nt(a, b):
    return lax.dot_general(a, b, (((1,), (1,)), ((), ())), preferred_element_type=F32)


def nn(a, b):
    return lax.dot_general(a, b, (((1,), (0,)), ((), ())), preferred_element_type=F32)


def split2(x):
    high = x.astype(BF16)
    low = (x - high.astype(F32)).astype(BF16)
    return jnp.concatenate([high, low], 0)


def halves(x):
    rows = x.shape[0] // 2
    return x[:rows] + x[rows:]


def turned(x):
    return pltpu.roll(x, LANES // 2, 1)


def kernel(
    n_mesh, n_samp,
    resid, u_in, c_in, stiff, diag, pattern, send_list, sizes,
    sol_out, res_out, coef_out,
    r, uc_loc, st, dg, stage, panel_send, panel_got, spread, cn, un,
    rb, t0, t1, r0t, send_a, send_m, got_a, got_m, w, wb, sol, coef_t,
    pay, rs_got, ar_got,
    in_sems, panel_ssem, panel_rsem, ghost_ssem, ghost_rsem, rs_ssem, rs_rsem, ag_ssem, ag_rsem, out_sems,
):
    me = lax.axis_index("mesh")
    mine = lax.axis_index("samp")
    cols, dofs = r.shape
    recy = cn.shape[0]
    rows_per = recy // n_samp
    quarters = 16 // rows_per
    wide = dofs // quarters // LANES
    pairs = dofs // PAIR
    stride = n_mesh // TILES
    live = sizes[0] * BLK
    low_half = lax.broadcasted_iota(jnp.int32, (cols, LANES), 1) < LANES // 2

    def row_alive(start, width):
        return (lax.broadcasted_iota(jnp.int32, (1, width), 1) + start) < live

    loads = [
        pltpu.make_async_copy(c_in, uc_loc.at[0], in_sems.at[0]),
        pltpu.make_async_copy(u_in, uc_loc.at[1], in_sems.at[1]),
        pltpu.make_async_copy(resid, r, in_sems.at[2]),
        pltpu.make_async_copy(diag, dg, in_sems.at[3]),
        pltpu.make_async_copy(stiff, st, in_sems.at[4]),
    ]
    for load in loads:
        load.start()

    barrier = pltpu.get_barrier_semaphore()

    def greet_mesh(o, carry):
        pl.semaphore_signal(barrier, inc=1, device_id={"mesh": lax.rem(me + o, n_mesh)}, device_id_type=MESH)
        return carry

    def greet_samp(o, carry):
        pl.semaphore_signal(barrier, inc=1, device_id={"samp": lax.rem(mine + o, n_samp)}, device_id_type=MESH)
        return carry

    lax.fori_loop(1, n_samp, greet_samp, 0)
    lax.fori_loop(1, n_mesh, greet_mesh, 0)

    def pack_panel(which):
        local = uc_loc[which].astype(F32)
        for q in range(quarters):
            for t in range(wide):
                at = (q * wide + t) * LANES
                stage[which, t, pl.ds(q, rows_per, stride=quarters), :] = local[:, at : at + LANES]
        packed = stage[which].astype(BF16)
        panel_send[which] = packed
        panel_got[which, mine] = packed

    def send_panel(which):
        def one(o, carry):
            pltpu.make_async_remote_copy(
                src_ref=panel_send.at[which],
                dst_ref=panel_got.at[which, mine],
                send_sem=panel_ssem.at[which],
                recv_sem=panel_rsem.at[which],
                device_id={"samp": lax.rem(mine + o, n_samp)},
                device_id_type=MESH,
            ).start()
            return carry

        lax.fori_loop(1, n_samp, one, 0)

    def wait_panel(which):
        others = panel_got.at[which, pl.ds(0, n_samp - 1)]
        pltpu.make_async_copy(others, others, panel_rsem.at[which]).wait()

    def panel_sent(which):
        others = panel_got.at[which, pl.ds(0, n_samp - 1)]
        pltpu.make_async_copy(others, others, panel_ssem.at[which]).wait()

    def natural(which, out):
        for k in range(n_samp):
            for t in range(wide):
                spread[t, 16 * k : 16 * k + 16, :] = panel_got[which, k, t].astype(F32)
        for q in range(quarters):
            for t in range(wide):
                at = (q * wide + t) * LANES
                tile = spread[t, pl.ds(q, recy, stride=quarters), :]
                out[:, at : at + LANES] = jnp.where(row_alive(at, LANES), tile, 0.0).astype(BF16)

    part = lax.div(me, stride)
    reducer = lax.rem(me, stride) == 0

    def rs_send(which, value):
        for t in range(TILES):
            pay[which, t] = value[8 * t : 8 * t + 8, :]

        @pl.when(reducer)
        def _():
            rs_got[which, me] = pay[which, part]

        def one(o, carry):
            t = lax.rem(part + o, TILES)
            target = t * stride

            @pl.when(target != me)
            def _():
                pltpu.make_async_remote_copy(
                    src_ref=pay.at[which, t],
                    dst_ref=rs_got.at[which, me],
                    send_sem=rs_ssem.at[which],
                    recv_sem=rs_rsem.at[which],
                    device_id={"mesh": target},
                    device_id_type=MESH,
                ).start()

            return carry

        lax.fori_loop(0, TILES, one, 0)

    def ag_send(which):
        @pl.when(reducer)
        def _():
            others = rs_got.at[which, pl.ds(0, n_mesh - 1)]
            pltpu.make_async_copy(others, others, rs_rsem.at[which]).wait()
            total = rs_got[which, 0]
            for d in range(1, n_mesh):
                total = total + rs_got[which, d]
            ar_got[which, part] = total

            def one(o, carry):
                pltpu.make_async_remote_copy(
                    src_ref=ar_got.at[which, part],
                    dst_ref=ar_got.at[which, part],
                    send_sem=ag_ssem.at[which],
                    recv_sem=ag_rsem.at[which],
                    device_id={"mesh": lax.rem(me + o, n_mesh)},
                    device_id_type=MESH,
                ).start()
                return carry

            lax.fori_loop(1, n_mesh, one, 0)

    def ar_wait(which):
        @pl.when(reducer)
        def _():
            some = ar_got.at[which, pl.ds(0, TILES - 1)]
            pltpu.make_async_copy(some, some, ag_rsem.at[which]).wait()

        @pl.when(jnp.logical_not(reducer))
        def _():
            pltpu.make_async_copy(ar_got.at[which], ar_got.at[which], ag_rsem.at[which]).wait()

        return jnp.concatenate([ar_got[which, t] for t in range(TILES)], 0)

    def ar_sent(which):
        @pl.when(reducer)
        def _():
            some = ar_got.at[which, pl.ds(0, TILES - 1)]
            pltpu.make_async_copy(some, some, rs_ssem.at[which]).wait()
            others = rs_got.at[which, pl.ds(0, n_mesh - 1)]
            pltpu.make_async_copy(others, others, ag_ssem.at[which]).wait()

        @pl.when(jnp.logical_not(reducer))
        def _():
            pltpu.make_async_copy(ar_got.at[which], ar_got.at[which], rs_ssem.at[which]).wait()

    def fill_tables(m, n0, n1, n2):
        b0, b1, b2 = n0.astype(BF16), n1.astype(BF16), n2.astype(BF16)
        v0, v1, v2 = turned(n0).astype(BF16), turned(n1).astype(BF16), turned(n2).astype(BF16)
        even, odd = 2 * m, 2 * m + 1
        t0[even] = b0
        r0t[even] = v0
        t1[even] = jnp.where(low_half, b1, v1)
        t0[odd] = jnp.where(low_half, v1, v2)
        r0t[odd] = jnp.where(low_half, b2, b1)
        t1[odd] = jnp.where(low_half, v2, b2)

    def ghost_copies(it):
        out = []
        for side, by in ((0, 1), (1, n_mesh - 1)):
            peer = {"mesh": lax.rem(me + by, n_mesh)}
            for j, (src, dst) in enumerate(((send_a, got_a), (send_m, got_m))):
                out.append(
                    pltpu.make_async_remote_copy(
                        src_ref=src.at[it, side],
                        dst_ref=dst.at[it, side],
                        send_sem=ghost_ssem.at[it, side, j],
                        recv_sem=ghost_rsem.at[it, side, j],
                        device_id=peer,
                        device_id_type=MESH,
                    )
                )
        return out

    def send_ghosts(it):
        ends = (me == n_mesh - 1, me == 0)
        for side in range(2):
            keep = jnp.where(ends[side], 0.0, 1.0).astype(BF16)
            for pair in range(GHOST // 2):
                a, b = send_list[side, 2 * pair], send_list[side, 2 * pair + 1]
                send_a[it, side, 2 * pair] = t0[a] * keep
                send_a[it, side, 2 * pair + 1] = t0[b] * keep
                send_m[it, side, pair] = jnp.where(low_half, t1[a], t1[b]) * keep
        copies = ghost_copies(it)
        for copy in copies:
            copy.start()

    def take_ghosts(it):
        for copy in ghost_copies(it):
            copy.wait()
        for side in range(2):
            base = 2 * pairs + side * GHOST
            for pair in range(GHOST // 2):
                for j in range(2):
                    x = got_a[it, side, 2 * pair + j]
                    t0[base + 2 * pair + j] = x
                    r0t[base + 2 * pair + j] = turned(x.astype(F32)).astype(BF16)
                x = got_m[it, side, pair]
                y = turned(x.astype(F32)).astype(BF16)
                t1[base + 2 * pair] = jnp.where(low_half, x, y)
                t1[base + 2 * pair + 1] = jnp.where(low_half, y, x)

    def gathered(i):
        parts = []
        for s in range(0, SLOTS, 2):
            a, b = pattern[i, s], pattern[i, s + 1]
            turned_b, tail_b = r0t[b], t1[b]
            parts.append(t0[a])
            parts.append(jnp.where(low_half, t1[a], turned_b))
            parts.append(jnp.where(low_half, turned_b, tail_b))
        return jnp.concatenate(parts, 1)

    def apply_stiff(it):
        def pair_step(m, carry):
            ww, wr = carry
            at = pl.multiple_of(m * PAIR, PAIR)
            out0 = nt(gathered(2 * m), st[pl.ds(at, 2 * LANES), :])
            out1 = nt(gathered(2 * m + 1), st[pl.ds(at + LANES, 2 * LANES), :])
            coupled = (
                out0[:, :LANES],
                jnp.where(low_half, out0[:, LANES:], out1[:, :LANES]),
                out1[:, LANES:],
            )
            for j in range(3):
                span = pl.ds(at + j * LANES, LANES)
                rounded = rb[it, :, span].astype(F32)
                image = jnp.where(
                    row_alive(at + j * LANES, LANES), dg[:, span] * rounded + coupled[j], 0.0
                )
                w[:, span] = image
                high = image.astype(BF16)
                wb[:cols, span] = high
                wb[cols:, span] = (image - high.astype(F32)).astype(BF16)
                ww = ww + image * image
                wr = wr + image * r[:, span]
            return ww, wr

        zero = jnp.zeros((cols, LANES), F32)
        ww, wr = lax.fori_loop(0, pairs, pair_step, (zero, zero))
        proj = halves(nt(wb[...], cn[...]))
        ww = jnp.sum(ww, axis=1, keepdims=True)
        wr = jnp.sum(wr, axis=1, keepdims=True)
        lane = lax.broadcasted_iota(jnp.int32, (cols, LANES - recy), 1)
        return jnp.concatenate([proj, jnp.where(lane == 0, ww, jnp.where(lane == 1, wr, 0.0))], 1)

    loads[0].wait()
    pack_panel(0)
    pl.semaphore_wait(barrier, n_mesh + n_samp - 2)
    send_panel(0)
    loads[1].wait()
    pack_panel(1)
    send_panel(1)
    loads[2].wait()
    for m in range(pairs):
        at = m * PAIR
        r[:, at : at + PAIR] = jnp.where(row_alive(at, PAIR), r[:, at : at + PAIR], 0.0)
        rb[0, :, at : at + PAIR] = r[:, at : at + PAIR].astype(BF16)
    wait_panel(0)
    natural(0, cn)
    first = nt(jnp.concatenate([rb[0], cn[...]], 0), cn[...])
    rs_send(0, jnp.concatenate([first[:cols], first[cols:]], 1))
    loads[3].wait()
    wait_panel(1)
    natural(1, un)
    loads[4].wait()
    ag_send(0)
    reduced = ar_wait(0)
    carried = reduced[:, :recy]
    gram = reduced[:, recy:]
    coef_t[...] = carried.T
    coef_copy = pltpu.make_async_copy(coef_t, coef_out, out_sems.at[0])
    coef_copy.start()
    highest = lax.Precision.HIGHEST
    c_r = carried - jnp.dot(carried, gram, precision=highest, preferred_element_type=F32)

    coef2 = split2(carried)

    def first_update(m, carry):
        span = pl.ds(pl.multiple_of(m * PAIR, PAIR), PAIR)
        new = r[:, span] - halves(nn(coef2, cn[:, span]))
        r[:, span] = new
        rb[0, :, span] = new.astype(BF16)
        fill_tables(m, new[:, :LANES], new[:, LANES : 2 * LANES], new[:, 2 * LANES :])
        return carry

    lax.fori_loop(0, pairs, first_update, 0)

    steps = []
    for it in range(ITERS):
        send_ghosts(it)
        take_ghosts(it)
        rs_send(it + 1, apply_stiff(it))
        ag_send(it + 1)
        reduced = ar_wait(it + 1)
        proj = reduced[:, :recy]
        ww = reduced[:, recy : recy + 1]
        wr = reduced[:, recy + 1 : recy + 2]
        p_gram = jnp.dot(proj, gram, precision=highest, preferred_element_type=F32)
        bottom = ww + jnp.sum(proj * (p_gram - 2.0 * proj), axis=1, keepdims=True)
        top = wr - jnp.sum(proj * c_r, axis=1, keepdims=True)
        step = top / bottom
        steps.append(step)
        c_r = c_r - step * (proj - p_gram)
        carried = carried - step * proj
        proj2 = split2(proj)
        if it + 1 < ITERS:

            def update(m, carry):
                span = pl.ds(pl.multiple_of(m * PAIR, PAIR), PAIR)
                new = r[:, span] - step * (w[:, span] - halves(nn(proj2, cn[:, span])))
                r[:, span] = new
                rb[it + 1, :, span] = new.astype(BF16)
                fill_tables(m, new[:, :LANES], new[:, LANES : 2 * LANES], new[:, 2 * LANES :])
                return carry

            lax.fori_loop(0, pairs, update, 0)
        else:
            carried2 = split2(carried)

            def finish(m, carry):
                span = pl.ds(pl.multiple_of(m * PAIR, PAIR), PAIR)
                r[:, span] = r[:, span] - step * (w[:, span] - halves(nn(proj2, cn[:, span])))
                direct = steps[0] * rb[0, :, span].astype(F32)
                for j in range(1, ITERS):
                    direct = direct + steps[j] * rb[j, :, span].astype(F32)
                sol[:, span] = halves(nn(carried2, un[:, span])) + direct
                return carry

            lax.fori_loop(0, pairs, finish, 0)

    outs = [
        coef_copy,
        pltpu.make_async_copy(r, res_out, out_sems.at[1]),
        pltpu.make_async_copy(sol, sol_out, out_sems.at[2]),
    ]
    for copy in outs[1:]:
        copy.start()
    for which in range(ITERS + 1):
        ar_sent(which)
    for which in range(2):
        panel_sent(which)
    for copy in outs:
        copy.wait()


def per_device(resid_in, recycle_u, recycle_c, stiff, diag_scale, pattern, send_list, part_sizes, n_mesh, n_samp):
    cols, dofs = resid_in.shape
    blocks, blk, width = stiff.shape
    recy = recycle_c.shape[0] * n_samp
    wide = dofs * recycle_c.shape[0] // 16 // LANES
    ext = blocks + 2 * GHOST
    hbm = pl.BlockSpec(memory_space=pl.ANY)
    smem = pl.BlockSpec(memory_space=pltpu.SMEM)
    dma = pltpu.SemaphoreType.DMA
    return pl.pallas_call(
        functools.partial(kernel, n_mesh, n_samp),
        out_shape=(
            jax.ShapeDtypeStruct((cols, dofs), F32),
            jax.ShapeDtypeStruct((cols, dofs), F32),
            jax.ShapeDtypeStruct((recy, cols), F32),
        ),
        in_specs=[hbm, hbm, hbm, hbm, hbm, smem, smem, smem],
        out_specs=(hbm, hbm, hbm),
        scratch_shapes=[
            pltpu.VMEM((cols, dofs), F32),
            pltpu.VMEM((2, recycle_c.shape[0], dofs), BF16),
            pltpu.VMEM((blocks * blk, width), BF16),
            pltpu.VMEM((1, dofs), F32),
            pltpu.VMEM((2, wide, 16, LANES), F32),
            pltpu.VMEM((2, wide, 16, LANES), BF16),
            pltpu.VMEM((2, n_samp, wide, 16, LANES), BF16),
            pltpu.VMEM((wide, 16 * n_samp, LANES), F32),
            pltpu.VMEM((recy, dofs), BF16),
            pltpu.VMEM((recy, dofs), BF16),
            pltpu.VMEM((ITERS, cols, dofs), BF16),
            pltpu.VMEM((ext, cols, LANES), BF16),
            pltpu.VMEM((ext, cols, LANES), BF16),
            pltpu.VMEM((ext, cols, LANES), BF16),
            pltpu.VMEM((ITERS, 2, GHOST, cols, LANES), BF16),
            pltpu.VMEM((ITERS, 2, GHOST // 2, cols, LANES), BF16),
            pltpu.VMEM((ITERS, 2, GHOST, cols, LANES), BF16),
            pltpu.VMEM((ITERS, 2, GHOST // 2, cols, LANES), BF16),
            pltpu.VMEM((cols, dofs), F32),
            pltpu.VMEM((2 * cols, dofs), BF16),
            pltpu.VMEM((cols, dofs), F32),
            pltpu.VMEM((recy, cols), F32),
            pltpu.VMEM((ITERS + 1, TILES, 8, LANES), F32),
            pltpu.VMEM((ITERS + 1, n_mesh, 8, LANES), F32),
            pltpu.VMEM((ITERS + 1, TILES, 8, LANES), F32),
            dma((5,)),
            dma((2,)),
            dma((2,)),
            dma((ITERS, 2, 2)),
            dma((ITERS, 2, 2)),
            dma((ITERS + 1,)),
            dma((ITERS + 1,)),
            dma((ITERS + 1,)),
            dma((ITERS + 1,)),
            dma((3,)),
        ],
        compiler_params=pltpu.CompilerParams(
            collective_id=0, has_side_effects=True, vmem_limit_bytes=48 << 20
        ),
    )(
        resid_in,
        recycle_u,
        recycle_c,
        stiff.reshape(blocks * blk, width),
        diag_scale.reshape(1, dofs),
        pattern,
        send_list,
        part_sizes,
    )


def solution(mesh):
    body = functools.partial(per_device, n_mesh=mesh.shape["mesh"], n_samp=mesh.shape["samp"])
    return jax.shard_map(
        body,
        mesh=mesh,
        in_specs=(
            P("samp", "mesh"),
            P("samp", "mesh"),
            P("samp", "mesh"),
            P("mesh", None, None),
            P("mesh"),
            P("mesh", None),
            P("mesh", None),
            P("mesh"),
        ),
        out_specs=(P("samp", "mesh"), P("samp", "mesh"), P(None, "samp")),
        check_vma=False,
    )
```

time: 505 us -> 106 us (0.21)
  blocking collectives: 414 us -> 0 us
  Pallas kernels: 0 us -> 96.9 us
  local copies, waits for them, and re-layouts: 44.8 us -> 7.13 us
  matrix products: 21.5 us -> 0 us
  starting transfers between devices: 11.8 us -> 0 us
  other arithmetic: 6.2 us -> 0 us
    psum x5 -> x0, blocking collectives: 375 us -> none  [the longest x2 181 us: per_device(): projected = lax.psum(local_proj, 'mesh')]
    pallas_call x0 -> x1, Pallas kernels: none -> 96.9 us  [per_device(): pl.pallas_call(functools.partial(kernel, n_mesh, n_samp), out_shape=(jax....]
    all_gather x2 -> x0, blocking collectives: 38.5 us -> none  [the longest x1 19.8 us: per_device(): lax.all_gather(recycle_c, 'samp', axis=0, tiled=True)]
    reshape x10 -> x0, local copies, waits for them, and re-layouts: 30.6 us -> none  [the longest x4 25.9 us: slot_product(): flat = picks.reshape(load_cols, stiff.shape[0], stiff.shape[2])]
    dot_general x9 -> x0, matrix products: 21.5 us -> none  [the longest x2 12.6 us: slot_product(): jnp.einsum('lik,ick->lic', flat, stiff, preferred_element_type=jnp.float32)]
    ppermute x4 -> x0, starting transfers between devices: 11.8 us -> none  [passed_along(): return lax.ppermute(x, axis, pairs)]
    gather x6 -> x0, local copies, waits for them, and re-layouts: 8.35 us -> none  [the longest x2 5.15 us: apply_stiff(): coupled = slot_product(extended[:, pattern], stiff)]
  transfers between devices with their start and end apart: 4 -> 0, of which waited for: 1 -> 0; matrix products, arithmetic and copies ran while one was open for 0% -> 0% of each run, Pallas kernels for 0% -> 0%
where the time goes in v1:
time: 106 us; the launch traced here: 105 us
  Pallas kernels  96.9 us (91%)
  local copies, waits for them, and re-layouts  7.13 us (7%)
  between operations  1.29 us (1%)
    pallas_call x1, Pallas kernels, per_device(): pl.pallas_call(functools.partial(kernel, n_mesh, n_samp), out_shape=(jax....  96.9 us
    unnamed x14, local copies, waits for them, and re-layouts  7.13 us

profile of v1, /device:TPU:1, one launch (start us, length us, event | category | flops | bytes accessed | tf_op | source)
XLA Modules:
  0.0 105.3 jit_solution(2832702984522085100)
XLA Ops:
  1.3 0.8 copy.11.pattern
  2.0 0.0 copy-start
  2.0 1.1 %copy-done = f32[64,3072]{1,0:T(8,128)S(1)} copy-done((f32[64,3072]{1,0:T(8,128)S(1)}, f32[64,3072]{1,0:T(8,128)}, u32[]{:S(2)}) %copy-start) | copy-done | bytes 786456
  3.2 0.0 copy-start.1
  3.2 0.7 copy-done.1
  3.9 0.0 copy-start.2
  3.9 0.7 copy-done.2
  4.7 0.0 copy-start.3
  4.7 0.7 copy-done.3
  5.4 0.0 copy-start.4
  5.4 0.7 copy-done.4
  6.0 96.9 %shard_map.103 = (f32[64,3072]{1,0:T(8,128)S(1)}, f32[64,3072]{1,0:T(8,128)S(1)}, f32[64,64]{1,0:T(8,128)S(1)}) custom-call(f32[64,3072]{1,0:T(8,128)S(1)} %copy-done, bf16[4,3072]{1,0:T(4,128)(2,1)S(1)} %copy-done.1, bf16[4,3072]{1,0:T(4,128)(2,1)S(1)} %copy-done.2, bf16[3072,1152]{1,0:T(8,128)(2,1)} %bitcast.3, f32[1,3072]{1,0:T(1,128)S(1)} %bitcast.2, ...), custom_call_target="tpu_custom_call" | custom-call | tf_op jit(solution)/shard_map/pallas_call | solution.py:419
  103.0 0.9 copy.16
  103.8 0.9 copy.17
  104.7 0.6 copy.18
Async XLA Ops:
  2.0 1.1 %copy-start = (f32[64,3072]{1,0:T(8,128)S(1)}, f32[64,3072]{1,0:T(8,128)}, u32[]{:S(2)}) copy-start(f32[64,3072]{1,0:T(8,128)} %resid.1) | copy-start | bytes 2359300
  3.2 0.7 copy-start.1
  3.9 0.7 copy-start.2
  4.7 0.7 copy-start.3
  5.4 0.7 copy-start.4

commit v2 on v1

v2 whole, which is shorter than its diff:
```python
import functools

import jax
import jax.numpy as jnp
from jax import lax
from jax.experimental import pallas as pl
from jax.experimental.pallas import tpu as pltpu
from jax.sharding import PartitionSpec as P

MESH = pl.DeviceIdType.MESH
F32 = jnp.float32
BF16 = jnp.bfloat16
LANES = 128
BLK = 192
PAIR = 2 * BLK
SLOTS = 6
GHOST = 8
ITERS = 2
TILES = 8


def nt(a, b):
    return lax.dot_general(a, b, (((1,), (1,)), ((), ())), preferred_element_type=F32)


def nn(a, b):
    return lax.dot_general(a, b, (((1,), (0,)), ((), ())), preferred_element_type=F32)


def split2(x):
    high = x.astype(BF16)
    low = (x - high.astype(F32)).astype(BF16)
    return jnp.concatenate([high, low], 0)


def halves(x):
    rows = x.shape[0] // 2
    return x[:rows] + x[rows:]


def turned(x):
    return pltpu.roll(x, LANES // 2, 1)


def kernel(
    n_mesh, n_samp,
    resid, u_in, c_in, stiff, diag, pattern_in, send_in, sizes_in,
    sol_out, res_out, coef_out,
    r, a, b, r_next, w_next, sol, coef_t,
    uc_loc, st, dg, pattern, send_list, sizes,
    stage, panel_send, panel_got, spread, cn, un, dn, rb, wb,
    t0, t1, r0t, send_f, got_f, send_c, got_c,
    pay, rs_got, ar_got,
    in_sems, panel_ssem, panel_rsem, ghost_ssem, ghost_rsem, rs_ssem, rs_rsem, ag_ssem, ag_rsem, out_sems,
):
    me = lax.axis_index("mesh")
    mine = lax.axis_index("samp")
    cols, dofs = r.shape
    recy = cn.shape[0]
    rows_per = recy // n_samp
    quarters = 16 // rows_per
    wide = dofs // quarters // LANES
    pairs = dofs // PAIR
    stride = n_mesh // TILES
    low_half = lax.broadcasted_iota(jnp.int32, (cols, LANES), 1) < LANES // 2
    highest = lax.Precision.HIGHEST

    loads = [
        pltpu.make_async_copy(src, dst, in_sems.at[i])
        for i, (src, dst) in enumerate(
            (
                (c_in, uc_loc.at[0]),
                (sizes_in, sizes),
                (resid, r),
                (send_in, send_list),
                (u_in, uc_loc.at[1]),
                (diag, dg),
                (pattern_in, pattern),
                (stiff, st),
            )
        )
    ]
    for load in loads:
        load.start()

    barrier = pltpu.get_barrier_semaphore()

    def greet_mesh(o, carry):
        pl.semaphore_signal(barrier, inc=1, device_id={"mesh": lax.rem(me + o, n_mesh)}, device_id_type=MESH)
        return carry

    def greet_samp(o, carry):
        pl.semaphore_signal(barrier, inc=1, device_id={"samp": lax.rem(mine + o, n_samp)}, device_id_type=MESH)
        return carry

    lax.fori_loop(1, n_mesh, greet_mesh, 0)
    lax.fori_loop(1, n_samp, greet_samp, 0)

    def row_alive(start, width):
        live = sizes[0] * BLK
        return (lax.broadcasted_iota(jnp.int32, (1, width), 1) + start) < live

    def pack_panel(which):
        local = uc_loc[which].astype(F32)
        for q in range(quarters):
            for t in range(wide):
                at = (q * wide + t) * LANES
                stage[which, t, pl.ds(q, rows_per, stride=quarters), :] = local[:, at : at + LANES]
        packed = stage[which].astype(BF16)
        panel_send[which] = packed
        panel_got[which, mine] = packed

    def send_panel(which):
        def one(o, carry):
            pltpu.make_async_remote_copy(
                src_ref=panel_send.at[which],
                dst_ref=panel_got.at[which, mine],
                send_sem=panel_ssem.at[which],
                recv_sem=panel_rsem.at[which],
                device_id={"samp": lax.rem(mine + o, n_samp)},
                device_id_type=MESH,
            ).start()
            return carry

        lax.fori_loop(1, n_samp, one, 0)

    def wait_panel(which, sems):
        others = panel_got.at[which, pl.ds(0, n_samp - 1)]
        pltpu.make_async_copy(others, others, sems.at[which]).wait()

    def natural(which, out):
        for k in range(n_samp):
            for t in range(wide):
                spread[t, 16 * k : 16 * k + 16, :] = panel_got[which, k, t].astype(F32)
        for q in range(quarters):
            for t in range(wide):
                at = (q * wide + t) * LANES
                tile = spread[t, pl.ds(q, recy, stride=quarters), :]
                out[:, at : at + LANES] = jnp.where(row_alive(at, LANES), tile, 0.0).astype(BF16)

    part = lax.div(me, stride)
    reducer = lax.rem(me, stride) == 0

    def rs_send(which, value):
        for t in range(TILES):
            pay[which, t] = value[8 * t : 8 * t + 8, :]

        @pl.when(reducer)
        def _():
            rs_got[which, me] = pay[which, part]

        def one(o, carry):
            t = lax.rem(part + o, TILES)
            target = t * stride

            @pl.when(target != me)
            def _():
                pltpu.make_async_remote_copy(
                    src_ref=pay.at[which, t],
                    dst_ref=rs_got.at[which, me],
                    send_sem=rs_ssem.at[which],
                    recv_sem=rs_rsem.at[which],
                    device_id={"mesh": target},
                    device_id_type=MESH,
                ).start()

            return carry

        lax.fori_loop(0, TILES, one, 0)

    def ag_send(which):
        @pl.when(reducer)
        def _():
            others = rs_got.at[which, pl.ds(0, n_mesh - 1)]
            pltpu.make_async_copy(others, others, rs_rsem.at[which]).wait()
            total = rs_got[which, 0]
            for d in range(1, n_mesh):
                total = total + rs_got[which, d]
            ar_got[which, part] = total

            def one(o, carry):
                pltpu.make_async_remote_copy(
                    src_ref=ar_got.at[which, part],
                    dst_ref=ar_got.at[which, part],
                    send_sem=ag_ssem.at[which],
                    recv_sem=ag_rsem.at[which],
                    device_id={"mesh": lax.rem(me + o, n_mesh)},
                    device_id_type=MESH,
                ).start()
                return carry

            lax.fori_loop(1, n_mesh, one, 0)

    def ar_wait(which):
        @pl.when(reducer)
        def _():
            some = ar_got.at[which, pl.ds(0, TILES - 1)]
            pltpu.make_async_copy(some, some, ag_rsem.at[which]).wait()

        @pl.when(jnp.logical_not(reducer))
        def _():
            pltpu.make_async_copy(ar_got.at[which], ar_got.at[which], ag_rsem.at[which]).wait()

        return jnp.concatenate([ar_got[which, t] for t in range(TILES)], 0)

    def ar_sent(which):
        @pl.when(reducer)
        def _():
            some = ar_got.at[which, pl.ds(0, TILES - 1)]
            pltpu.make_async_copy(some, some, rs_ssem.at[which]).wait()
            others = rs_got.at[which, pl.ds(0, n_mesh - 1)]
            pltpu.make_async_copy(others, others, ag_ssem.at[which]).wait()

        @pl.when(jnp.logical_not(reducer))
        def _():
            pltpu.make_async_copy(ar_got.at[which], ar_got.at[which], rs_ssem.at[which]).wait()

    def fill_tables(m, row, tiles):
        n0, n1, n2 = tiles
        b0, b1, b2 = n0.astype(BF16), n1.astype(BF16), n2.astype(BF16)
        v0, v1, v2 = turned(n0).astype(BF16), turned(n1).astype(BF16), turned(n2).astype(BF16)
        even, odd, rows = 2 * m, 2 * m + 1, slice(row, row + cols)
        t0[even, rows] = b0
        r0t[even, rows] = v0
        t1[even, rows] = jnp.where(low_half, b1, v1)
        t0[odd, rows] = jnp.where(low_half, v1, v2)
        r0t[odd, rows] = jnp.where(low_half, b2, b1)
        t1[odd, rows] = jnp.where(low_half, v2, b2)

    def fill_split(source):
        def one(m, carry):
            at = pl.multiple_of(m * PAIR, PAIR)
            tiles = [source[:, pl.ds(at + j * LANES, LANES)] for j in range(3)]
            fill_tables(m, 0, tiles)
            fill_tables(m, cols, [x - x.astype(BF16).astype(F32) for x in tiles])
            return carry

        lax.fori_loop(0, pairs, one, 0)

    def ghost_copies(send, got, which):
        out = []
        for side, by in ((0, 1), (1, n_mesh - 1)):
            out.append(
                pltpu.make_async_remote_copy(
                    src_ref=send.at[side],
                    dst_ref=got.at[side],
                    send_sem=ghost_ssem.at[which, side],
                    recv_sem=ghost_rsem.at[which, side],
                    device_id={"mesh": lax.rem(me + by, n_mesh)},
                    device_id_type=MESH,
                )
            )
        return out

    def pack_ghosts(send, row, rows):
        ends = (me == n_mesh - 1, me == 0)
        for side in range(2):
            keep = jnp.where(ends[side], 0.0, 1.0).astype(BF16)
            for start in range(0, rows, cols):
                span, to = slice(row + start, row + start + cols), slice(start, start + cols)
                for pair in range(GHOST // 2):
                    x, y = send_list[side, 2 * pair], send_list[side, 2 * pair + 1]
                    send[side, 2 * pair, to] = t0[x, span] * keep
                    send[side, 2 * pair + 1, to] = t0[y, span] * keep
                    send[side, GHOST + pair, to] = jnp.where(low_half, t1[x, span], t1[y, span]) * keep

    def take_ghosts(got, row, rows):
        for side in range(2):
            base = 2 * pairs + side * GHOST
            for start in range(0, rows, cols):
                span, to = slice(start, start + cols), slice(row + start, row + start + cols)
                for pair in range(GHOST // 2):
                    for j in range(2):
                        x = got[side, 2 * pair + j, span]
                        t0[base + 2 * pair + j, to] = x
                        r0t[base + 2 * pair + j, to] = turned(x.astype(F32)).astype(BF16)
                    x = got[side, GHOST + pair, span]
                    y = turned(x.astype(F32)).astype(BF16)
                    t1[base + 2 * pair, to] = jnp.where(low_half, x, y)
                    t1[base + 2 * pair + 1, to] = jnp.where(low_half, y, x)

    def apply_stiff(rows, emit):
        low_rows = lax.broadcasted_iota(jnp.int32, (rows, LANES), 1) < LANES // 2

        def gathered(i):
            parts = []
            for s in range(0, SLOTS, 2):
                x, y = pattern[i, s], pattern[i, s + 1]
                turned_y = r0t[y, :rows]
                parts.append(t0[x, :rows])
                parts.append(jnp.where(low_rows, t1[x, :rows], turned_y))
                parts.append(jnp.where(low_rows, turned_y, t1[y, :rows]))
            return jnp.concatenate(parts, 1)

        def one(m, carry):
            at = pl.multiple_of(m * PAIR, PAIR)
            out0 = nt(gathered(2 * m), st[pl.ds(at, 2 * LANES), :])
            out1 = nt(gathered(2 * m + 1), st[pl.ds(at + LANES, 2 * LANES), :])
            emit(at, 0, out0[:, :LANES])
            emit(at, 1, jnp.where(low_rows, out0[:, LANES:], out1[:, :LANES]))
            emit(at, 2, out1[:, LANES:])
            return carry

        lax.fori_loop(0, pairs, one, 0)

    def emit_first(at, j, value):
        span = pl.ds(at + j * LANES, LANES)
        keep, scale = row_alive(at + j * LANES, LANES), dg[:, span]
        a[:, span] = jnp.where(keep, halves(value[: 2 * cols]) + scale * r[:, span], 0.0)
        dn[:, span] = jnp.where(keep, value[2 * cols :] + scale * cn[:, span].astype(F32), 0.0).astype(BF16)

    def emit_second(at, j, value):
        span = pl.ds(at + j * LANES, LANES)
        b[:, span] = jnp.where(
            row_alive(at + j * LANES, LANES), halves(value) + dg[:, span] * a[:, span], 0.0
        )

    def renew(make, r_to, w_to):
        def one(m, carry):
            ww, wr = carry
            at = pl.multiple_of(m * PAIR, PAIR)
            span = pl.ds(at, PAIR)
            new_r, image = make(span)
            r_to[:, span] = new_r
            w_to[:, span] = image
            high = image.astype(BF16)
            wb[:cols, span] = high
            wb[cols:, span] = (image - high.astype(F32)).astype(BF16)
            for j in range(3):
                x = image[:, j * LANES : (j + 1) * LANES]
                ww = ww + x * x
                wr = wr + x * new_r[:, j * LANES : (j + 1) * LANES]
            return ww, wr

        zero = jnp.zeros((cols, LANES), F32)
        ww, wr = lax.fori_loop(0, pairs, one, (zero, zero))
        proj = halves(nt(wb[...], cn[...]))
        ww = jnp.sum(ww, axis=1, keepdims=True)
        wr = jnp.sum(wr, axis=1, keepdims=True)
        lane = lax.broadcasted_iota(jnp.int32, (cols, LANES - recy), 1)
        return jnp.concatenate([proj, jnp.where(lane == 0, ww, jnp.where(lane == 1, wr, 0.0))], 1)

    def step_of(reduced, c_r):
        proj = reduced[:, :recy]
        ww = reduced[:, recy : recy + 1]
        wr = reduced[:, recy + 1 : recy + 2]
        p_gram = jnp.dot(proj, gram, precision=highest, preferred_element_type=F32)
        bottom = ww + jnp.sum(proj * (p_gram - 2.0 * proj), axis=1, keepdims=True)
        top = wr - jnp.sum(proj * c_r, axis=1, keepdims=True)
        step = top / bottom
        return proj, step, c_r - step * (proj - p_gram)

    loads[0].wait()
    pack_panel(0)
    loads[1].wait()
    loads[2].wait()

    def mask(m, carry):
        at = pl.multiple_of(m * PAIR, PAIR)
        span = pl.ds(at, PAIR)
        kept = jnp.where(row_alive(at, PAIR), r[:, span], 0.0)
        r[:, span] = kept
        rb[:, span] = kept.astype(BF16)
        return carry

    lax.fori_loop(0, pairs, mask, 0)
    fill_split(r)
    loads[3].wait()
    pack_ghosts(send_f.at[0], 0, 2 * cols)
    loads[4].wait()
    pack_panel(1)
    pl.semaphore_wait(barrier, n_mesh + n_samp - 2)
    send_panel(0)
    for copy in ghost_copies(send_f.at[0], got_f.at[0], 0):
        copy.start()
    send_panel(1)
    wait_panel(0, panel_rsem)
    natural(0, cn)
    first = nt(jnp.concatenate([rb[...], cn[...]], 0), cn[...])
    rs_send(0, jnp.concatenate([first[:cols], first[cols:]], 1))

    def fill_panel(m, carry):
        at = pl.multiple_of(m * PAIR, PAIR)
        fill_tables(m, 2 * cols, [cn[:, pl.ds(at + j * LANES, LANES)].astype(F32) for j in range(3)])
        return carry

    lax.fori_loop(0, pairs, fill_panel, 0)
    pack_ghosts(send_c, 2 * cols, recy)
    for copy in ghost_copies(send_c, got_c, 1):
        copy.start()
    for copy in ghost_copies(send_f.at[0], got_f.at[0], 0):
        copy.wait()
    take_ghosts(got_f.at[0], 0, 2 * cols)
    wait_panel(1, panel_rsem)
    natural(1, un)
    for load in loads[5:]:
        load.wait()
    for copy in ghost_copies(send_c, got_c, 1):
        copy.wait()
    take_ghosts(got_c, 2 * cols, recy)
    ag_send(0)
    apply_stiff(2 * cols + recy, emit_first)
    reduced = ar_wait(0)
    coef = reduced[:, :recy]
    gram = reduced[:, recy:]
    coef2 = split2(coef)

    def make_first(span):
        new_r = r[:, span] - halves(nn(coef2, cn[:, span]))
        return new_r, a[:, span] - halves(nn(coef2, dn[:, span]))

    rs_send(1, renew(make_first, r, a))

    coef_t[...] = coef.T
    coef_copy = pltpu.make_async_copy(coef_t, coef_out, out_sems.at[0])
    coef_copy.start()
    c_r = coef - jnp.dot(coef, gram, precision=highest, preferred_element_type=F32)
    fill_split(a)
    pack_ghosts(send_f.at[1], 0, 2 * cols)
    for copy in ghost_copies(send_f.at[1], got_f.at[1], 2):
        copy.start()
    for copy in ghost_copies(send_f.at[1], got_f.at[1], 2):
        copy.wait()
    take_ghosts(got_f.at[1], 0, 2 * cols)
    ag_send(1)
    apply_stiff(2 * cols, emit_second)
    proj, step1, c_r = step_of(ar_wait(1), c_r)
    proj2 = split2(proj)

    def make_second(span):
        image = a[:, span]
        new_r = r[:, span] - step1 * (image - halves(nn(proj2, cn[:, span])))
        return new_r, image - step1 * (b[:, span] - halves(nn(proj2, dn[:, span])))

    rs_send(2, renew(make_second, r_next, w_next))

    carried2 = split2(coef - step1 * proj)

    def base(m, carry):
        span = pl.ds(pl.multiple_of(m * PAIR, PAIR), PAIR)
        rounded = r[:, span].astype(BF16).astype(F32)
        sol[:, span] = halves(nn(carried2, un[:, span])) + step1 * rounded
        return carry

    lax.fori_loop(0, pairs, base, 0)
    ag_send(2)
    proj, step2, _ = step_of(ar_wait(2), c_r)
    proj2 = split2(proj)

    def finish(m, carry):
        span = pl.ds(pl.multiple_of(m * PAIR, PAIR), PAIR)
        old = r_next[:, span]
        r[:, span] = old - step2 * (w_next[:, span] - halves(nn(proj2, cn[:, span])))
        rounded = old.astype(BF16).astype(F32)
        sol[:, span] = sol[:, span] + step2 * (rounded - halves(nn(proj2, un[:, span])))
        return carry

    lax.fori_loop(0, pairs, finish, 0)
    outs = [
        coef_copy,
        pltpu.make_async_copy(r, res_out, out_sems.at[1]),
        pltpu.make_async_copy(sol, sol_out, out_sems.at[2]),
    ]
    for copy in outs[1:]:
        copy.start()
    for which in range(ITERS + 1):
        ar_sent(which)
    for which in range(2):
        wait_panel(which, panel_ssem)
    for copy in outs:
        copy.wait()


def per_device(resid_in, recycle_u, recycle_c, stiff, diag_scale, pattern, send_list, part_sizes, n_mesh, n_samp):
    cols, dofs = resid_in.shape
    blocks, blk, width = stiff.shape
    recy = recycle_c.shape[0] * n_samp
    wide = dofs * recycle_c.shape[0] // 16 // LANES
    ext = blocks + 2 * GHOST
    hbm = pl.BlockSpec(memory_space=pltpu.HBM)
    dma = pltpu.SemaphoreType.DMA
    field = pltpu.VMEM((cols, dofs), F32)
    panel = pltpu.VMEM((recy, dofs), BF16)
    table = pltpu.VMEM((ext, 2 * cols + recy, LANES), BF16)
    return pl.pallas_call(
        functools.partial(kernel, n_mesh, n_samp),
        out_shape=(
            jax.ShapeDtypeStruct((cols, dofs), F32),
            jax.ShapeDtypeStruct((cols, dofs), F32),
            jax.ShapeDtypeStruct((recy, cols), F32),
        ),
        in_specs=[hbm] * 8,
        out_specs=(hbm, hbm, hbm),
        scratch_shapes=[
            field,
            field,
            field,
            field,
            field,
            field,
            pltpu.VMEM((recy, cols), F32),
            pltpu.VMEM((2, recycle_c.shape[0], dofs), BF16),
            pltpu.VMEM((blocks * blk, width), BF16),
            pltpu.VMEM((1, dofs), F32),
            pltpu.SMEM(pattern.shape, jnp.int32),
            pltpu.SMEM(send_list.shape, jnp.int32),
            pltpu.SMEM(part_sizes.shape, jnp.int32),
            pltpu.VMEM((2, wide, 16, LANES), F32),
            pltpu.VMEM((2, wide, 16, LANES), BF16),
            pltpu.VMEM((2, n_samp, wide, 16, LANES), BF16),
            pltpu.VMEM((wide, 16 * n_samp, LANES), F32),
            panel,
            panel,
            panel,
            pltpu.VMEM((cols, dofs), BF16),
            pltpu.VMEM((2 * cols, dofs), BF16),
            table,
            table,
            table,
            pltpu.VMEM((ITERS, 2, GHOST + GHOST // 2, 2 * cols, LANES), BF16),
            pltpu.VMEM((ITERS, 2, GHOST + GHOST // 2, 2 * cols, LANES), BF16),
            pltpu.VMEM((2, GHOST + GHOST // 2, recy, LANES), BF16),
            pltpu.VMEM((2, GHOST + GHOST // 2, recy, LANES), BF16),
            pltpu.VMEM((ITERS + 1, TILES, 8, LANES), F32),
            pltpu.VMEM((ITERS + 1, n_mesh, 8, LANES), F32),
            pltpu.VMEM((ITERS + 1, TILES, 8, LANES), F32),
            dma((8,)),
            dma((2,)),
            dma((2,)),
            dma((ITERS + 1, 2)),
            dma((ITERS + 1, 2)),
            dma((ITERS + 1,)),
            dma((ITERS + 1,)),
            dma((ITERS + 1,)),
            dma((ITERS + 1,)),
            dma((3,)),
        ],
        compiler_params=pltpu.CompilerParams(
            collective_id=0, has_side_effects=True, vmem_limit_bytes=56 << 20
        ),
    )(
        resid_in,
        recycle_u,
        recycle_c,
        stiff.reshape(blocks * blk, width),
        diag_scale.reshape(1, dofs),
        pattern,
        send_list,
        part_sizes,
    )


def solution(mesh):
    body = functools.partial(per_device, n_mesh=mesh.shape["mesh"], n_samp=mesh.shape["samp"])
    return jax.shard_map(
        body,
        mesh=mesh,
        in_specs=(
            P("samp", "mesh"),
            P("samp", "mesh"),
            P("samp", "mesh"),
            P("mesh", None, None),
            P("mesh"),
            P("mesh", None),
            P("mesh", None),
            P("mesh"),
        ),
        out_specs=(P("samp", "mesh"), P("samp", "mesh"), P(None, "samp")),
        check_vma=False,
    )
```

time: 106 us -> 87.9 us (0.83)
  Pallas kernels: 96.9 us -> 79.4 us
    pallas_call x1, Pallas kernels: 96.9 us -> 79.4 us  [per_device(): pl.pallas_call(functools.partial(kernel, n_mesh, n_samp), out_shape=(jax....]
    unnamed x14 -> x4, local copies, waits for them, and re-layouts: 7.13 us -> 6.87 us
where the time goes in v2:
time: 87.9 us; the launch traced here: 87.6 us
  Pallas kernels  79.4 us (90%)
  local copies, waits for them, and re-layouts  6.87 us (8%)
  between operations  1.29 us (1%)
    pallas_call x1, Pallas kernels, per_device(): pl.pallas_call(functools.partial(kernel, n_mesh, n_samp), out_shape=(jax....  79.4 us
    unnamed x4, local copies, waits for them, and re-layouts  6.87 us

profile of v2, /device:TPU:1, one launch (start us, length us, event | category | flops | bytes accessed | tf_op | source)
XLA Modules:
  0.0 87.6 jit_solution(16766353361158424323)
XLA Ops:
  1.3 1.4 %copy.11.pattern_in = s32[16,6]{1,0:T(8,128)} copy(s32[16,6]{0,1:T(8,128)} %param.13) | data formatting | bytes 768 | tf_op args[5]
  2.6 79.4 %shard_map.103 = (f32[64,3072]{1,0:T(8,128)}, f32[64,3072]{1,0:T(8,128)}, f32[64,64]{1,0:T(8,128)}) custom-call(f32[64,3072]{1,0:T(8,128)} %resid.1, bf16[4,3072]{1,0:T(4,128)(2,1)} %u_in.1, bf16[4,3072]{1,0:T(4,128)(2,1)} %c_in.1, bf16[3072,1152]{1,0:T(8,128)(2,1)} %bitcast.2, f32[1,3072]{1,0:T(1,128)} %bitcast.3, s32[16,6]{1,0:T(8,128)} %copy.11.pattern_in, ...), custom_call_target="tpu_custom_call" | custom-call | tf_op jit(solution)/shard_map/pallas_call | solution.py:485
  82.1 2.1 %copy.16 = f32[64,3072]{1,0:T(8,128)} copy(f32[64,3072]{1,0:T(8,128)} %get-tuple-element.6) | data formatting | bytes 1572864
  84.2 2.1 %copy.17 = f32[64,3072]{1,0:T(8,128)} copy(f32[64,3072]{1,0:T(8,128)} %get-tuple-element.7) | data formatting | bytes 1572864
  86.2 1.4 %copy.18 = f32[64,64]{1,0:T(8,128)} copy(f32[64,64]{1,0:T(8,128)} %get-tuple-element.8) | data formatting | bytes 32768

commit v3 on v2

--- a/solution.py
+++ b/solution.py
@@ -28,9 +28,8 @@
 
 
 def split2(x):
-    high = x.astype(BF16)
-    low = (x - high.astype(F32)).astype(BF16)
-    return jnp.concatenate([high, low], 0)
+    high = x.astype(BF16).astype(F32)
+    return jnp.concatenate([high, x - high], 1).astype(BF16)
 
 
 def halves(x):
@@ -46,22 +45,21 @@
     n_mesh, n_samp,
     resid, u_in, c_in, stiff, diag, pattern_in, send_in, sizes_in,
     sol_out, res_out, coef_out,
-    r, a, b, r_next, w_next, sol, coef_t,
+    r, a, b, r_next, w_next,
     uc_loc, st, dg, pattern, send_list, sizes,
     stage, panel_send, panel_got, spread, cn, un, dn, rb, wb,
     t0, t1, r0t, send_f, got_f, send_c, got_c,
     pay, rs_got, ar_got,
-    in_sems, panel_ssem, panel_rsem, ghost_ssem, ghost_rsem, rs_ssem, rs_rsem, ag_ssem, ag_rsem, out_sems,
+    in_sems, panel_ssem, panel_rsem, ghost_ssem, ghost_rsem, rs_ssem, rs_rsem, ag_ssem, ag_rsem,
 ):
     me = lax.axis_index("mesh")
     mine = lax.axis_index("samp")
     cols, dofs = r.shape
-    recy = cn.shape[0]
+    recy = cn.shape[0] // 2
     rows_per = recy // n_samp
     quarters = 16 // rows_per
     wide = dofs // quarters // LANES
     pairs = dofs // PAIR
-    stride = n_mesh // TILES
     low_half = lax.broadcasted_iota(jnp.int32, (cols, LANES), 1) < LANES // 2
     highest = lax.Precision.HIGHEST
 
@@ -136,84 +134,96 @@
             for t in range(wide):
                 at = (q * wide + t) * LANES
                 tile = spread[t, pl.ds(q, recy, stride=quarters), :]
-                out[:, at : at + LANES] = jnp.where(row_alive(at, LANES), tile, 0.0).astype(BF16)
-
-    part = lax.div(me, stride)
-    reducer = lax.rem(me, stride) == 0
+                tile = jnp.where(row_alive(at, LANES), tile, 0.0).astype(BF16)
+                out[:recy, at : at + LANES] = tile
+                out[recy:, at : at + LANES] = tile
+
+    chips = n_mesh // 2
+    span = chips // 2
+    chip, core = lax.div(me, 2), lax.rem(me, 2)
+    part = lax.rem(chip, span)
+    reducer = core == lax.rem(part, 2)
+    own_sum = lax.div(chip, span) * TILES + part
+    all_sums = 2 * TILES
 
     def rs_send(which, value):
         for t in range(TILES):
             pay[which, t] = value[8 * t : 8 * t + 8, :]
 
-        @pl.when(reducer)
-        def _():
-            rs_got[which, me] = pay[which, part]
-
-        def one(o, carry):
-            t = lax.rem(part + o, TILES)
-            target = t * stride
+        def one(t, carry):
+            away = lax.rem(chip - t + chips + span // 2 - 1, chips)
+            slot = 2 * lax.rem(away, span) + core
+            target = 2 * lax.rem(t + span * lax.div(away, span), chips) + lax.rem(t, 2)
 
             @pl.when(target != me)
             def _():
                 pltpu.make_async_remote_copy(
                     src_ref=pay.at[which, t],
-                    dst_ref=rs_got.at[which, me],
+                    dst_ref=rs_got.at[which, slot],
                     send_sem=rs_ssem.at[which],
                     recv_sem=rs_rsem.at[which],
                     device_id={"mesh": target},
                     device_id_type=MESH,
                 ).start()
 
+            @pl.when(target == me)
+            def _():
+                rs_got[which, slot] = pay[which, t]
+
             return carry
 
         lax.fori_loop(0, TILES, one, 0)
+
+    def tiles_done(sem, count):
+        some = ar_got.at[pl.ds(0, count)]
+        pltpu.make_async_copy(some, some, sem).wait()
 
     def ag_send(which):
         @pl.when(reducer)
         def _():
-            others = rs_got.at[which, pl.ds(0, n_mesh - 1)]
-            pltpu.make_async_copy(others, others, rs_rsem.at[which]).wait()
+            tiles_done(rs_rsem.at[which], 2 * span - 1)
             total = rs_got[which, 0]
-            for d in range(1, n_mesh):
+            for d in range(1, 2 * span):
                 total = total + rs_got[which, d]
-            ar_got[which, part] = total
+            at = which * all_sums + own_sum
+            ar_got[at] = total
 
             def one(o, carry):
+                half = lax.div(o + 1, 2)
+                ahead = n_mesh // 2 + half * (1 - 2 * lax.rem(o, 2))
                 pltpu.make_async_remote_copy(
-                    src_ref=ar_got.at[which, part],
-                    dst_ref=ar_got.at[which, part],
+                    src_ref=ar_got.at[at],
+                    dst_ref=ar_got.at[at],
                     send_sem=ag_ssem.at[which],
                     recv_sem=ag_rsem.at[which],
-                    device_id={"mesh": lax.rem(me + o, n_mesh)},
+                    device_id={"mesh": lax.rem(me + ahead, n_mesh)},
                     device_id_type=MESH,
                 ).start()
                 return carry
 
-            lax.fori_loop(1, n_mesh, one, 0)
+            lax.fori_loop(0, n_mesh - 1, one, 0)
 
     def ar_wait(which):
         @pl.when(reducer)
         def _():
-            some = ar_got.at[which, pl.ds(0, TILES - 1)]
-            pltpu.make_async_copy(some, some, ag_rsem.at[which]).wait()
+            tiles_done(ag_rsem.at[which], all_sums - 1)
 
         @pl.when(jnp.logical_not(reducer))
         def _():
-            pltpu.make_async_copy(ar_got.at[which], ar_got.at[which], ag_rsem.at[which]).wait()
-
-        return jnp.concatenate([ar_got[which, t] for t in range(TILES)], 0)
+            tiles_done(ag_rsem.at[which], all_sums)
+
+        at = which * all_sums
+        return jnp.concatenate([ar_got[at + t] + ar_got[at + TILES + t] for t in range(TILES)], 0)
 
     def ar_sent(which):
         @pl.when(reducer)
         def _():
-            some = ar_got.at[which, pl.ds(0, TILES - 1)]
-            pltpu.make_async_copy(some, some, rs_ssem.at[which]).wait()
-            others = rs_got.at[which, pl.ds(0, n_mesh - 1)]
-            pltpu.make_async_copy(others, others, ag_ssem.at[which]).wait()
+            tiles_done(rs_ssem.at[which], TILES - 1)
+            tiles_done(ag_ssem.at[which], n_mesh - 1)
 
         @pl.when(jnp.logical_not(reducer))
         def _():
-            pltpu.make_async_copy(ar_got.at[which], ar_got.at[which], rs_ssem.at[which]).wait()
+            tiles_done(rs_ssem.at[which], TILES)
 
     def fill_tables(m, row, tiles):
         n0, n1, n2 = tiles
@@ -285,7 +295,7 @@
         def gathered(i):
             parts = []
             for s in range(0, SLOTS, 2):
-                x, y = pattern[i, s], pattern[i, s + 1]
+                x, y = pattern[s, i], pattern[s + 1, i]
                 turned_y = r0t[y, :rows]
                 parts.append(t0[x, :rows])
                 parts.append(jnp.where(low_rows, t1[x, :rows], turned_y))
@@ -307,7 +317,10 @@
         span = pl.ds(at + j * LANES, LANES)
         keep, scale = row_alive(at + j * LANES, LANES), dg[:, span]
         a[:, span] = jnp.where(keep, halves(value[: 2 * cols]) + scale * r[:, span], 0.0)
-        dn[:, span] = jnp.where(keep, value[2 * cols :] + scale * cn[:, span].astype(F32), 0.0).astype(BF16)
+        image = value[2 * cols :] + scale * cn[:recy, span].astype(F32)
+        image = jnp.where(keep, image, 0.0).astype(BF16)
+        dn[:recy, span] = image
+        dn[recy:, span] = image
 
     def emit_second(at, j, value):
         span = pl.ds(at + j * LANES, LANES)
@@ -333,8 +346,8 @@
             return ww, wr
 
         zero = jnp.zeros((cols, LANES), F32)
-        ww, wr = lax.fori_loop(0, pairs, one, (zero, zero))
-        proj = halves(nt(wb[...], cn[...]))
+        ww, wr = lax.fori_loop(0, pairs, one, (zero, zero), unroll=4)
+        proj = halves(nt(wb[...], cn[:recy]))
         ww = jnp.sum(ww, axis=1, keepdims=True)
         wr = jnp.sum(wr, axis=1, keepdims=True)
         lane = lax.broadcasted_iota(jnp.int32, (cols, LANES - recy), 1)
@@ -373,15 +386,15 @@
     send_panel(0)
     for copy in ghost_copies(send_f.at[0], got_f.at[0], 0):
         copy.start()
-    send_panel(1)
     wait_panel(0, panel_rsem)
     natural(0, cn)
-    first = nt(jnp.concatenate([rb[...], cn[...]], 0), cn[...])
+    first = nt(jnp.concatenate([rb[...], cn[:recy]], 0), cn[:recy])
     rs_send(0, jnp.concatenate([first[:cols], first[cols:]], 1))
 
+    send_panel(1)
     def fill_panel(m, carry):
         at = pl.multiple_of(m * PAIR, PAIR)
-        fill_tables(m, 2 * cols, [cn[:, pl.ds(at + j * LANES, LANES)].astype(F32) for j in range(3)])
+        fill_tables(m, 2 * cols, [cn[:recy, pl.ds(at + j * LANES, LANES)].astype(F32) for j in range(3)])
         return carry
 
     lax.fori_loop(0, pairs, fill_panel, 0)
@@ -391,14 +404,12 @@
     for copy in ghost_copies(send_f.at[0], got_f.at[0], 0):
         copy.wait()
     take_ghosts(got_f.at[0], 0, 2 * cols)
-    wait_panel(1, panel_rsem)
-    natural(1, un)
     for load in loads[5:]:
         load.wait()
+    ag_send(0)
     for copy in ghost_copies(send_c, got_c, 1):
         copy.wait()
     take_ghosts(got_c, 2 * cols, recy)
-    ag_send(0)
     apply_stiff(2 * cols + recy, emit_first)
     reduced = ar_wait(0)
     coef = reduced[:, :recy]
@@ -406,31 +417,31 @@
     coef2 = split2(coef)
 
     def make_first(span):
-        new_r = r[:, span] - halves(nn(coef2, cn[:, span]))
-        return new_r, a[:, span] - halves(nn(coef2, dn[:, span]))
+        new_r = r[:, span] - nn(coef2, cn[:, span])
+        return new_r, a[:, span] - nn(coef2, dn[:, span])
 
     rs_send(1, renew(make_first, r, a))
 
-    coef_t[...] = coef.T
-    coef_copy = pltpu.make_async_copy(coef_t, coef_out, out_sems.at[0])
-    coef_copy.start()
+    coef_out[...] = coef.T
     c_r = coef - jnp.dot(coef, gram, precision=highest, preferred_element_type=F32)
     fill_split(a)
     pack_ghosts(send_f.at[1], 0, 2 * cols)
     for copy in ghost_copies(send_f.at[1], got_f.at[1], 2):
         copy.start()
+    wait_panel(1, panel_rsem)
+    natural(1, un)
+    ag_send(1)
     for copy in ghost_copies(send_f.at[1], got_f.at[1], 2):
         copy.wait()
     take_ghosts(got_f.at[1], 0, 2 * cols)
-    ag_send(1)
     apply_stiff(2 * cols, emit_second)
     proj, step1, c_r = step_of(ar_wait(1), c_r)
     proj2 = split2(proj)
 
     def make_second(span):
         image = a[:, span]
-        new_r = r[:, span] - step1 * (image - halves(nn(proj2, cn[:, span])))
-        return new_r, image - step1 * (b[:, span] - halves(nn(proj2, dn[:, span])))
+        new_r = r[:, span] - step1 * (image - nn(proj2, cn[:, span]))
+        return new_r, image - step1 * (b[:, span] - nn(proj2, dn[:, span]))
 
     rs_send(2, renew(make_second, r_next, w_next))
 
@@ -439,10 +450,10 @@
     def base(m, carry):
         span = pl.ds(pl.multiple_of(m * PAIR, PAIR), PAIR)
         rounded = r[:, span].astype(BF16).astype(F32)
-        sol[:, span] = halves(nn(carried2, un[:, span])) + step1 * rounded
+        sol_out[:, span] = nn(carried2, un[:, span]) + step1 * rounded
         return carry
 
-    lax.fori_loop(0, pairs, base, 0)
+    lax.fori_loop(0, pairs, base, 0, unroll=2)
     ag_send(2)
     proj, step2, _ = step_of(ar_wait(2), c_r)
     proj2 = split2(proj)
@@ -450,25 +461,16 @@
     def finish(m, carry):
         span = pl.ds(pl.multiple_of(m * PAIR, PAIR), PAIR)
         old = r_next[:, span]
-        r[:, span] = old - step2 * (w_next[:, span] - halves(nn(proj2, cn[:, span])))
+        res_out[:, span] = old - step2 * (w_next[:, span] - nn(proj2, cn[:, span]))
         rounded = old.astype(BF16).astype(F32)
-        sol[:, span] = sol[:, span] + step2 * (rounded - halves(nn(proj2, un[:, span])))
+        sol_out[:, span] = sol_out[:, span] + step2 * (rounded - nn(proj2, un[:, span]))
         return carry
 
-    lax.fori_loop(0, pairs, finish, 0)
-    outs = [
-        coef_copy,
-        pltpu.make_async_copy(r, res_out, out_sems.at[1]),
-        pltpu.make_async_copy(sol, sol_out, out_sems.at[2]),
-    ]
-    for copy in outs[1:]:
-        copy.start()
+    lax.fori_loop(0, pairs, finish, 0, unroll=4)
     for which in range(ITERS + 1):
         ar_sent(which)
     for which in range(2):
         wait_panel(which, panel_ssem)
-    for copy in outs:
-        copy.wait()
 
 
 def per_device(resid_in, recycle_u, recycle_c, stiff, diag_scale, pattern, send_list, part_sizes, n_mesh, n_samp):
@@ -478,9 +480,10 @@
     wide = dofs * recycle_c.shape[0] // 16 // LANES
     ext = blocks + 2 * GHOST
     hbm = pl.BlockSpec(memory_space=pltpu.HBM)
+    vmem = pl.BlockSpec(memory_space=pltpu.VMEM)
     dma = pltpu.SemaphoreType.DMA
     field = pltpu.VMEM((cols, dofs), F32)
-    panel = pltpu.VMEM((recy, dofs), BF16)
+    panel = pltpu.VMEM((2 * recy, dofs), BF16)
     table = pltpu.VMEM((ext, 2 * cols + recy, LANES), BF16)
     return pl.pallas_call(
         functools.partial(kernel, n_mesh, n_samp),
@@ -490,19 +493,17 @@
             jax.ShapeDtypeStruct((recy, cols), F32),
         ),
         in_specs=[hbm] * 8,
-        out_specs=(hbm, hbm, hbm),
+        out_specs=(vmem, vmem, vmem),
         scratch_shapes=[
             field,
             field,
             field,
             field,
             field,
-            field,
-            pltpu.VMEM((recy, cols), F32),
             pltpu.VMEM((2, recycle_c.shape[0], dofs), BF16),
             pltpu.VMEM((blocks * blk, width), BF16),
             pltpu.VMEM((1, dofs), F32),
-            pltpu.SMEM(pattern.shape, jnp.int32),
+            pltpu.SMEM(pattern.shape[::-1], jnp.int32),
             pltpu.SMEM(send_list.shape, jnp.int32),
             pltpu.SMEM(part_sizes.shape, jnp.int32),
             pltpu.VMEM((2, wide, 16, LANES), F32),
@@ -522,8 +523,8 @@
             pltpu.VMEM((2, GHOST + GHOST // 2, recy, LANES), BF16),
             pltpu.VMEM((2, GHOST + GHOST // 2, recy, LANES), BF16),
             pltpu.VMEM((ITERS + 1, TILES, 8, LANES), F32),
-            pltpu.VMEM((ITERS + 1, n_mesh, 8, LANES), F32),
-            pltpu.VMEM((ITERS + 1, TILES, 8, LANES), F32),
+            pltpu.VMEM((ITERS + 1, n_mesh // 2, 8, LANES), F32),
+            pltpu.VMEM(((ITERS + 1) * 2 * TILES, 8, LANES), F32),
             dma((8,)),
             dma((2,)),
             dma((2,)),
@@ -533,10 +534,9 @@
             dma((ITERS + 1,)),
             dma((ITERS + 1,)),
             dma((ITERS + 1,)),
-            dma((3,)),
         ],
         compiler_params=pltpu.CompilerParams(
-            collective_id=0, has_side_effects=True, vmem_limit_bytes=56 << 20
+            collective_id=0, has_side_effects=True, vmem_limit_bytes=62 << 20
         ),
     )(
         resid_in,
@@ -544,7 +544,7 @@
         recycle_c,
         stiff.reshape(blocks * blk, width),
         diag_scale.reshape(1, dofs),
-        pattern,
+        pattern.T,
         send_list,
         part_sizes,
     )

time: 87.9 us -> 75.8 us (0.86)
  Pallas kernels: 79.4 us -> 68.7 us
  local copies, waits for them, and re-layouts: 6.87 us -> 5.51 us
    pallas_call x1, Pallas kernels: 79.4 us -> 68.7 us  [per_device(): pl.pallas_call(functools.partial(kernel, n_mesh, n_samp), out_shape=(jax....]
    unnamed x4 -> x3, local copies, waits for them, and re-layouts: 6.87 us -> 5.51 us
where the time goes in v3:
time: 75.8 us; the launch traced here: 75.5 us
  Pallas kernels  68.7 us (91%)
  local copies, waits for them, and re-layouts  5.51 us (7%)
  between operations  1.29 us (2%)
    pallas_call x1, Pallas kernels, per_device(): pl.pallas_call(functools.partial(kernel, n_mesh, n_samp), out_shape=(jax....  68.7 us
    unnamed x3, local copies, waits for them, and re-layouts  5.51 us

profile of v3, /device:TPU:1, one launch (start us, length us, event | category | flops | bytes accessed | tf_op | source)
XLA Modules:
  0.0 75.5 jit_solution(15676861900254312870)
XLA Ops:
  1.3 68.7 %shard_map.103 = (f32[64,3072]{1,0:T(8,128)}, f32[64,3072]{1,0:T(8,128)}, f32[64,64]{1,0:T(8,128)}) custom-call(f32[64,3072]{1,0:T(8,128)} %resid.1, bf16[4,3072]{1,0:T(4,128)(2,1)} %u_in.1, bf16[4,3072]{1,0:T(4,128)(2,1)} %c_in.1, bf16[3072,1152]{1,0:T(8,128)(2,1)} %bitcast.3, f32[1,3072]{1,0:T(1,128)} %bitcast.4, s32[6,16]{1,0:T(8,128)} %bitcast.5, ...), custom_call_target="tpu_custom_call" | custom-call | tf_op jit(solution)/shard_map/pallas_call | solution.py:488
  70.0 2.1 %copy.15 = f32[64,3072]{1,0:T(8,128)} copy(f32[64,3072]{1,0:T(8,128)} %get-tuple-element.6) | data formatting | bytes 1572864
  72.1 2.1 %copy.16 = f32[64,3072]{1,0:T(8,128)} copy(f32[64,3072]{1,0:T(8,128)} %get-tuple-element.7) | data formatting | bytes 1572864
  74.2 1.4 %copy.17 = f32[64,64]{1,0:T(8,128)} copy(f32[64,64]{1,0:T(8,128)} %get-tuple-element.8) | data formatting | bytes 32768

commit v4 on v3

--- a/solution.py
+++ b/solution.py
@@ -17,6 +17,8 @@
 GHOST = 8
 ITERS = 2
 TILES = 8
+REACH = 4
+PARTS = 4
 
 
 def nt(a, b):
@@ -44,13 +46,13 @@
 def kernel(
     n_mesh, n_samp,
     resid, u_in, c_in, stiff, diag, pattern_in, send_in, sizes_in,
-    sol_out, res_out, coef_out,
-    r, a, b, r_next, w_next,
+    r_out, w_out, base_out, cn_out, un_out, fin_out, coef_out,
+    r, a, b, r_next, w_next, base_sol, fin, coef_t, own,
     uc_loc, st, dg, pattern, send_list, sizes,
     stage, panel_send, panel_got, spread, cn, un, dn, rb, wb,
     t0, t1, r0t, send_f, got_f, send_c, got_c,
     pay, rs_got, ar_got,
-    in_sems, panel_ssem, panel_rsem, ghost_ssem, ghost_rsem, rs_ssem, rs_rsem, ag_ssem, ag_rsem,
+    in_sems, panel_ssem, panel_rsem, ghost_ssem, ghost_rsem, rs_ssem, rs_rsem, ag_ssem, ag_rsem, out_sems, far_sem,
 ):
     me = lax.axis_index("mesh")
     mine = lax.axis_index("samp")
@@ -82,16 +84,23 @@
         load.start()
 
     barrier = pltpu.get_barrier_semaphore()
+    chips = n_mesh // 2
+    chip, core = lax.div(me, 2), lax.rem(me, 2)
 
     def greet_mesh(o, carry):
-        pl.semaphore_signal(barrier, inc=1, device_id={"mesh": lax.rem(me + o, n_mesh)}, device_id_type=MESH)
+        peer = 2 * lax.rem(chip + chips - REACH + lax.div(o, 2), chips) + lax.rem(o, 2)
+
+        @pl.when(peer != me)
+        def _():
+            pl.semaphore_signal(barrier, inc=1, device_id={"mesh": peer}, device_id_type=MESH)
+
         return carry
 
     def greet_samp(o, carry):
         pl.semaphore_signal(barrier, inc=1, device_id={"samp": lax.rem(mine + o, n_samp)}, device_id_type=MESH)
         return carry
 
-    lax.fori_loop(1, n_mesh, greet_mesh, 0)
+    lax.fori_loop(0, 4 * REACH + 2, greet_mesh, 0)
     lax.fori_loop(1, n_samp, greet_samp, 0)
 
     def row_alive(start, width):
@@ -138,9 +147,7 @@
                 out[:recy, at : at + LANES] = tile
                 out[recy:, at : at + LANES] = tile
 
-    chips = n_mesh // 2
     span = chips // 2
-    chip, core = lax.div(me, 2), lax.rem(me, 2)
     part = lax.rem(chip, span)
     reducer = core == lax.rem(part, 2)
     own_sum = lax.div(chip, span) * TILES + part
@@ -262,7 +269,7 @@
             )
         return out
 
-    def pack_ghosts(send, row, rows):
+    def pack_ghosts(send, row, rows, copies=()):
         ends = (me == n_mesh - 1, me == 0)
         for side in range(2):
             keep = jnp.where(ends[side], 0.0, 1.0).astype(BF16)
@@ -273,6 +280,8 @@
                     send[side, 2 * pair, to] = t0[x, span] * keep
                     send[side, 2 * pair + 1, to] = t0[y, span] * keep
                     send[side, GHOST + pair, to] = jnp.where(low_half, t1[x, span], t1[y, span]) * keep
+            if copies:
+                copies[side].start()
 
     def take_ghosts(got, row, rows):
         for side in range(2):
@@ -289,29 +298,49 @@
                     t1[base + 2 * pair, to] = jnp.where(low_half, x, y)
                     t1[base + 2 * pair + 1, to] = jnp.where(low_half, y, x)
 
+    def by_pairs(rows, low_rows, lanes, left, emit):
+        def one(m, carry):
+            at = pl.multiple_of(m * PAIR, PAIR)
+            out0 = nt(left(2 * m), st[pl.ds(at, 2 * LANES), lanes])
+            out1 = nt(left(2 * m + 1), st[pl.ds(at + LANES, 2 * LANES), lanes])
+            emit(at, 0, out0[:, :LANES])
+            emit(at, 1, jnp.where(low_rows, out0[:, LANES:], out1[:, :LANES]))
+            emit(at, 2, out1[:, LANES:])
+            return carry
+
+        lax.fori_loop(0, pairs, one, 0)
+
+    def apply_own(rows):
+        low_rows = lax.broadcasted_iota(jnp.int32, (rows, LANES), 1) < LANES // 2
+        none = jnp.zeros((rows, LANES), BF16)
+
+        def left(i):
+            return jnp.concatenate([t0[i, :rows], jnp.where(low_rows, t1[i, :rows], none)], 1)
+
+        def emit(at, j, value):
+            own[:rows, pl.ds(at + j * LANES, LANES)] = value
+
+        by_pairs(rows, low_rows, slice(0, 2 * LANES), left, emit)
+
     def apply_stiff(rows, emit):
         low_rows = lax.broadcasted_iota(jnp.int32, (rows, LANES), 1) < LANES // 2
-
-        def gathered(i):
+        none = jnp.zeros((rows, LANES), BF16)
+
+        def left(i):
             parts = []
             for s in range(0, SLOTS, 2):
                 x, y = pattern[s, i], pattern[s + 1, i]
                 turned_y = r0t[y, :rows]
-                parts.append(t0[x, :rows])
-                parts.append(jnp.where(low_rows, t1[x, :rows], turned_y))
+                if s:
+                    parts.append(t0[x, :rows])
+                parts.append(jnp.where(low_rows, t1[x, :rows] if s else none, turned_y))
                 parts.append(jnp.where(low_rows, turned_y, t1[y, :rows]))
             return jnp.concatenate(parts, 1)
 
-        def one(m, carry):
-            at = pl.multiple_of(m * PAIR, PAIR)
-            out0 = nt(gathered(2 * m), st[pl.ds(at, 2 * LANES), :])
-            out1 = nt(gathered(2 * m + 1), st[pl.ds(at + LANES, 2 * LANES), :])
-            emit(at, 0, out0[:, :LANES])
-            emit(at, 1, jnp.where(low_rows, out0[:, LANES:], out1[:, :LANES]))
-            emit(at, 2, out1[:, LANES:])
-            return carry
-
-        lax.fori_loop(0, pairs, one, 0)
+        def whole(at, j, value):
+            emit(at, j, value + own[:rows, pl.ds(at + j * LANES, LANES)])
+
+        by_pairs(rows, low_rows, slice(LANES, SLOTS * BLK), left, whole)
 
     def emit_first(at, j, value):
         span = pl.ds(at + j * LANES, LANES)
@@ -382,7 +411,10 @@
     pack_ghosts(send_f.at[0], 0, 2 * cols)
     loads[4].wait()
     pack_panel(1)
-    pl.semaphore_wait(barrier, n_mesh + n_samp - 2)
+    pl.semaphore_wait(barrier, 4 * REACH + n_samp)
+    for by in (REACH, chips - REACH):
+        peer = 2 * lax.rem(chip + by, chips) + core
+        pl.semaphore_signal(far_sem, inc=1, device_id={"mesh": peer}, device_id_type=MESH)
     send_panel(0)
     for copy in ghost_copies(send_f.at[0], got_f.at[0], 0):
         copy.start()
@@ -398,14 +430,14 @@
         return carry
 
     lax.fori_loop(0, pairs, fill_panel, 0)
-    pack_ghosts(send_c, 2 * cols, recy)
-    for copy in ghost_copies(send_c, got_c, 1):
-        copy.start()
+    pack_ghosts(send_c, 2 * cols, recy, ghost_copies(send_c, got_c, 1))
     for copy in ghost_copies(send_f.at[0], got_f.at[0], 0):
         copy.wait()
     take_ghosts(got_f.at[0], 0, 2 * cols)
     for load in loads[5:]:
         load.wait()
+    apply_own(2 * cols + recy)
+    pl.semaphore_wait(far_sem, 2)
     ag_send(0)
     for copy in ghost_copies(send_c, got_c, 1):
         copy.wait()
@@ -422,12 +454,11 @@
 
     rs_send(1, renew(make_first, r, a))
 
-    coef_out[...] = coef.T
+    coef_t[...] = coef.T
     c_r = coef - jnp.dot(coef, gram, precision=highest, preferred_element_type=F32)
     fill_split(a)
-    pack_ghosts(send_f.at[1], 0, 2 * cols)
-    for copy in ghost_copies(send_f.at[1], got_f.at[1], 2):
-        copy.start()
+    pack_ghosts(send_f.at[1], 0, 2 * cols, ghost_copies(send_f.at[1], got_f.at[1], 2))
+    apply_own(2 * cols)
     wait_panel(1, panel_rsem)
     natural(1, un)
     ag_send(1)
@@ -450,27 +481,81 @@
     def base(m, carry):
         span = pl.ds(pl.multiple_of(m * PAIR, PAIR), PAIR)
         rounded = r[:, span].astype(BF16).astype(F32)
-        sol_out[:, span] = nn(carried2, un[:, span]) + step1 * rounded
+        base_sol[:, span] = nn(carried2, un[:, span]) + step1 * rounded
         return carry
 
     lax.fori_loop(0, pairs, base, 0, unroll=2)
+    outs = [
+        pltpu.make_async_copy(src, dst, out_sems.at[i])
+        for i, (src, dst) in enumerate(
+            (
+                (r_next, r_out),
+                (w_next, w_out),
+                (base_sol, base_out),
+                (cn.at[:recy], cn_out),
+                (un.at[:recy], un_out),
+                (coef_t, coef_out),
+                (fin, fin_out),
+            )
+        )
+    ]
+    for copy in outs[:6]:
+        copy.start()
+    for which in range(2):
+        wait_panel(which, panel_ssem)
+        ar_sent(which)
     ag_send(2)
     proj, step2, _ = step_of(ar_wait(2), c_r)
-    proj2 = split2(proj)
-
-    def finish(m, carry):
-        span = pl.ds(pl.multiple_of(m * PAIR, PAIR), PAIR)
-        old = r_next[:, span]
-        res_out[:, span] = old - step2 * (w_next[:, span] - nn(proj2, cn[:, span]))
+    fin[...] = jnp.concatenate([proj, jnp.broadcast_to(step2, (cols, LANES - recy))], 1)
+    outs[6].start()
+    ar_sent(2)
+    for copy in outs:
+        copy.wait()
+
+def last_kernel(
+    r_in, w_in, base_in, cn_in, un_in, fin_in, coef_in,
+    sol_out, res_out, coef_out,
+    r, w, sol, cn, un, fin, in_sems, out_sems,
+):
+    cols, dofs = r.shape
+    recy = cn.shape[0]
+    width = dofs // PARTS
+    coef_copy = pltpu.make_async_copy(coef_in, coef_out, out_sems.at[0, 0])
+    coef_copy.start()
+    fin_copy = pltpu.make_async_copy(fin_in, fin, out_sems.at[0, 1])
+    fin_copy.start()
+    loads, outs = [], []
+    for i in range(PARTS):
+        span = pl.ds(i * width, width)
+        pairs = ((cn_in, cn), (w_in, w), (r_in, r), (un_in, un), (base_in, sol))
+        loads.append(
+            [
+                pltpu.make_async_copy(src.at[:, span], dst.at[:, span], in_sems.at[i, j])
+                for j, (src, dst) in enumerate(pairs)
+            ]
+        )
+        for load in loads[-1]:
+            load.start()
+    fin_copy.wait()
+    proj, step = fin[:, :recy], fin[:, recy : recy + 1]
+    high = proj.astype(BF16)
+    proj2 = jnp.concatenate([high, (proj - high.astype(F32)).astype(BF16)], 0)
+    for i in range(PARTS):
+        for load in loads[i]:
+            load.wait()
+        at = slice(i * width, (i + 1) * width)
+        old = r[:, at]
+        r[:, at] = old - step * (w[:, at] - halves(nn(proj2, cn[:, at])))
         rounded = old.astype(BF16).astype(F32)
-        sol_out[:, span] = sol_out[:, span] + step2 * (rounded - nn(proj2, un[:, span]))
-        return carry
-
-    lax.fori_loop(0, pairs, finish, 0, unroll=4)
-    for which in range(ITERS + 1):
-        ar_sent(which)
-    for which in range(2):
-        wait_panel(which, panel_ssem)
+        sol[:, at] = sol[:, at] + step * (rounded - halves(nn(proj2, un[:, at])))
+        for j, (src, dst) in enumerate(((r, res_out), (sol, sol_out))):
+            span = pl.ds(i * width, width)
+            out = pltpu.make_async_copy(src.at[:, span], dst.at[:, span], out_sems.at[i + 1, j])
+            out.start()
+            outs.append(out)
+    coef_copy.wait()
+    for out in outs:
+        out.wait()
 
 
 def per_device(resid_in, recycle_u, recycle_c, stiff, diag_scale, pattern, send_list, part_sizes, n_mesh, n_samp):
@@ -480,26 +565,33 @@
     wide = dofs * recycle_c.shape[0] // 16 // LANES
     ext = blocks + 2 * GHOST
     hbm = pl.BlockSpec(memory_space=pltpu.HBM)
-    vmem = pl.BlockSpec(memory_space=pltpu.VMEM)
     dma = pltpu.SemaphoreType.DMA
     field = pltpu.VMEM((cols, dofs), F32)
     panel = pltpu.VMEM((2 * recy, dofs), BF16)
     table = pltpu.VMEM((ext, 2 * cols + recy, LANES), BF16)
-    return pl.pallas_call(
+    middle = pl.pallas_call(
         functools.partial(kernel, n_mesh, n_samp),
         out_shape=(
             jax.ShapeDtypeStruct((cols, dofs), F32),
             jax.ShapeDtypeStruct((cols, dofs), F32),
+            jax.ShapeDtypeStruct((cols, dofs), F32),
+            jax.ShapeDtypeStruct((recy, dofs), BF16),
+            jax.ShapeDtypeStruct((recy, dofs), BF16),
+            jax.ShapeDtypeStruct((cols, LANES), F32),
             jax.ShapeDtypeStruct((recy, cols), F32),
         ),
         in_specs=[hbm] * 8,
-        out_specs=(vmem, vmem, vmem),
+        out_specs=(hbm,) * 7,
         scratch_shapes=[
             field,
             field,
             field,
             field,
             field,
+            field,
+            pltpu.VMEM((cols, LANES), F32),
+            pltpu.VMEM((recy, cols), F32),
+            pltpu.VMEM((2 * cols + recy, dofs), F32),
             pltpu.VMEM((2, recycle_c.shape[0], dofs), BF16),
             pltpu.VMEM((blocks * blk, width), BF16),
             pltpu.VMEM((1, dofs), F32),
@@ -534,6 +626,8 @@
             dma((ITERS + 1,)),
             dma((ITERS + 1,)),
             dma((ITERS + 1,)),
+            dma((7,)),
+            pltpu.SemaphoreType.REGULAR,
         ],
         compiler_params=pltpu.CompilerParams(
             collective_id=0, has_side_effects=True, vmem_limit_bytes=62 << 20
@@ -548,6 +642,28 @@
         send_list,
         part_sizes,
     )
+    plain = pltpu.VMEM((recy, dofs), BF16)
+    return pl.pallas_call(
+        last_kernel,
+        out_shape=(
+            jax.ShapeDtypeStruct((cols, dofs), F32),
+            jax.ShapeDtypeStruct((cols, dofs), F32),
+            jax.ShapeDtypeStruct((recy, cols), F32),
+        ),
+        in_specs=[hbm] * 7,
+        out_specs=(hbm,) * 3,
+        scratch_shapes=[
+            field,
+            field,
+            field,
+            plain,
+            plain,
+            pltpu.VMEM((cols, LANES), F32),
+            dma((PARTS, 5)),
+            dma((PARTS + 1, 2)),
+        ],
+        compiler_params=pltpu.CompilerParams(vmem_limit_bytes=62 << 20),
+    )(*middle)
 
 
 def solution(mesh):

time: 75.8 us -> 68.7 us (0.906)
  local copies, waits for them, and re-layouts: 5.51 us -> 0 us
  Pallas kernels: 68.7 us -> 67.3 us
    unnamed x3 -> x0, local copies, waits for them, and re-layouts: 5.51 us -> none
    pallas_call x1, Pallas kernels: 68.7 us -> 63.5 us  [per_device(): pl.pallas_call(functools.partial(kernel, n_mesh, n_samp), out_shape=(jax....]
    pallas_call x0 -> x1, Pallas kernels: none -> 3.75 us  [per_device(): pl.pallas_call(last_kernel, out_shape=(jax.ShapeDtypeStruct((cols, dofs),...]
where the time goes in v4:
time: 68.7 us; the launch traced here: 68.6 us
  Pallas kernels  67.3 us (98%)
  between operations  1.29 us (2%)
    pallas_call x1, Pallas kernels, per_device(): pl.pallas_call(functools.partial(kernel, n_mesh, n_samp), out_shape=(jax....  63.5 us
    pallas_call x1, Pallas kernels, per_device(): pl.pallas_call(last_kernel, out_shape=(jax.ShapeDtypeStruct((cols, dofs),...  3.75 us

profile of v4, /device:TPU:1, one launch (start us, length us, event | category | flops | bytes accessed | tf_op | source)
XLA Modules:
  0.0 68.6 jit_solution(3908327543755728756)
XLA Ops:
  1.3 63.5 %shard_map.103 = (f32[64,3072]{1,0:T(8,128)}, f32[64,3072]{1,0:T(8,128)}, f32[64,3072]{1,0:T(8,128)}, bf16[64,3072]{1,0:T(8,128)(2,1)}, bf16[64,3072]{1,0:T(8,12...) custom-call(f32[64,3072]{1,0:T(8,128)} %resid.1, bf16[4,3072]{1,0:T(4,128)(2,1)} %u_in.1, bf16[4,3072]{1,0:T(4,128)(2,1)} %c_in.1, ...), custom_call_target="tpu_custom_call" | custom-call | tf_op jit(solution)/shard_map/pallas_call | solution.py:572
  64.8 3.8 %shard_map.104 = (f32[64,3072]{1,0:T(8,128)}, f32[64,3072]{1,0:T(8,128)}, f32[64,64]{1,0:T(8,128)}) custom-call(f32[64,3072]{1,0:T(8,128)} %get-tuple-element.10.r_in, f32[64,3072]{1,0:T(8,128)} %get-tuple-element.11.w_in, f32[64,3072]{1,0:T(8,128)} %get-tuple-element.12.base_in, bf16[64,3072]{1,0:T(8,128)(2,1)} %get-tuple-element.13.cn_in, ...), custom_call_target="tpu_custom_call" | custom-call | tf_op jit(solution)/shard_map/pallas_call | solution.py:646

commit v5 on v4

--- a/solution.py
+++ b/solution.py
@@ -18,7 +18,8 @@
 ITERS = 2
 TILES = 8
 REACH = 4
-PARTS = 4
+SQUARE = 4
+PARTS = 2
 
 
 def nt(a, b):
@@ -46,7 +47,7 @@
 def kernel(
     n_mesh, n_samp,
     resid, u_in, c_in, stiff, diag, pattern_in, send_in, sizes_in,
-    r_out, w_out, base_out, cn_out, un_out, fin_out, coef_out,
+    fields_out, panels_out, fin_out, coef_out,
     r, a, b, r_next, w_next, base_sol, fin, coef_t, own,
     uc_loc, st, dg, pattern, send_list, sizes,
     stage, panel_send, panel_got, spread, cn, un, dn, rb, wb,
@@ -87,21 +88,23 @@
     chips = n_mesh // 2
     chip, core = lax.div(me, 2), lax.rem(me, 2)
 
-    def greet_mesh(o, carry):
-        peer = 2 * lax.rem(chip + chips - REACH + lax.div(o, 2), chips) + lax.rem(o, 2)
-
-        @pl.when(peer != me)
-        def _():
-            pl.semaphore_signal(barrier, inc=1, device_id={"mesh": peer}, device_id_type=MESH)
-
-        return carry
-
-    def greet_samp(o, carry):
-        pl.semaphore_signal(barrier, inc=1, device_id={"samp": lax.rem(mine + o, n_samp)}, device_id_type=MESH)
-        return carry
-
-    lax.fori_loop(0, 4 * REACH + 2, greet_mesh, 0)
-    lax.fori_loop(1, n_samp, greet_samp, 0)
+    side = SQUARE
+    row, column = lax.div(mine, side), lax.rem(mine, side)
+    ring = [min(k, side - k) for k in range(side)]
+    hops = sorted(range(1, n_samp), key=lambda o: -(ring[o // side] + ring[o % side]))
+    peers = [side * lax.rem(row + o // side, side) + lax.rem(column + o % side, side) for o in hops]
+
+    def greet(**device):
+        pl.semaphore_signal(barrier, inc=1, device_id=device, device_id_type=MESH)
+
+    for away in range(REACH, 0, -1):
+        for by in (away, chips - away):
+            for which in range(2):
+                greet(mesh=2 * lax.rem(chip + by, chips) + which)
+        if away == REACH:
+            for peer in peers:
+                greet(samp=peer)
+    greet(mesh=2 * chip + 1 - core)
 
     def row_alive(start, width):
         live = sizes[0] * BLK
@@ -118,18 +121,15 @@
         panel_got[which, mine] = packed
 
     def send_panel(which):
-        def one(o, carry):
+        for peer in peers:
             pltpu.make_async_remote_copy(
                 src_ref=panel_send.at[which],
                 dst_ref=panel_got.at[which, mine],
                 send_sem=panel_ssem.at[which],
                 recv_sem=panel_rsem.at[which],
-                device_id={"samp": lax.rem(mine + o, n_samp)},
+                device_id={"samp": peer},
                 device_id_type=MESH,
             ).start()
-            return carry
-
-        lax.fori_loop(1, n_samp, one, 0)
 
     def wait_panel(which, sems):
         others = panel_got.at[which, pl.ds(0, n_samp - 1)]
@@ -252,7 +252,7 @@
             fill_tables(m, cols, [x - x.astype(BF16).astype(F32) for x in tiles])
             return carry
 
-        lax.fori_loop(0, pairs, one, 0)
+        lax.fori_loop(0, pairs, one, 0, unroll=2)
 
     def ghost_copies(send, got, which):
         out = []
@@ -308,7 +308,7 @@
             emit(at, 2, out1[:, LANES:])
             return carry
 
-        lax.fori_loop(0, pairs, one, 0)
+        lax.fori_loop(0, pairs, one, 0, unroll=4)
 
     def apply_own(rows):
         low_rows = lax.broadcasted_iota(jnp.int32, (rows, LANES), 1) < LANES // 2
@@ -394,6 +394,11 @@
 
     loads[0].wait()
     pack_panel(0)
+    pl.semaphore_wait(barrier, 4 * REACH + n_samp)
+    for by in (REACH, chips - REACH):
+        peer = 2 * lax.rem(chip + by, chips) + core
+        pl.semaphore_signal(far_sem, inc=1, device_id={"mesh": peer}, device_id_type=MESH)
+    send_panel(0)
     loads[1].wait()
     loads[2].wait()
 
@@ -408,16 +413,9 @@
     lax.fori_loop(0, pairs, mask, 0)
     fill_split(r)
     loads[3].wait()
-    pack_ghosts(send_f.at[0], 0, 2 * cols)
+    pack_ghosts(send_f.at[0], 0, 2 * cols, ghost_copies(send_f.at[0], got_f.at[0], 0))
     loads[4].wait()
     pack_panel(1)
-    pl.semaphore_wait(barrier, 4 * REACH + n_samp)
-    for by in (REACH, chips - REACH):
-        peer = 2 * lax.rem(chip + by, chips) + core
-        pl.semaphore_signal(far_sem, inc=1, device_id={"mesh": peer}, device_id_type=MESH)
-    send_panel(0)
-    for copy in ghost_copies(send_f.at[0], got_f.at[0], 0):
-        copy.start()
     wait_panel(0, panel_rsem)
     natural(0, cn)
     first = nt(jnp.concatenate([rb[...], cn[:recy]], 0), cn[:recy])
@@ -429,7 +427,7 @@
         fill_tables(m, 2 * cols, [cn[:recy, pl.ds(at + j * LANES, LANES)].astype(F32) for j in range(3)])
         return carry
 
-    lax.fori_loop(0, pairs, fill_panel, 0)
+    lax.fori_loop(0, pairs, fill_panel, 0, unroll=2)
     pack_ghosts(send_c, 2 * cols, recy, ghost_copies(send_c, got_c, 1))
     for copy in ghost_copies(send_f.at[0], got_f.at[0], 0):
         copy.wait()
@@ -489,11 +487,11 @@
         pltpu.make_async_copy(src, dst, out_sems.at[i])
         for i, (src, dst) in enumerate(
             (
-                (r_next, r_out),
-                (w_next, w_out),
-                (base_sol, base_out),
-                (cn.at[:recy], cn_out),
-                (un.at[:recy], un_out),
+                (r_next, fields_out.at[0]),
+                (w_next, fields_out.at[1]),
+                (base_sol, fields_out.at[2]),
+                (cn.at[:recy], panels_out.at[0]),
+                (un.at[:recy], panels_out.at[1]),
                 (coef_t, coef_out),
                 (fin, fin_out),
             )
@@ -513,29 +511,28 @@
         copy.wait()
 
 def last_kernel(
-    r_in, w_in, base_in, cn_in, un_in, fin_in, coef_in,
+    fields_in, panels_in, fin_in, coef_in,
     sol_out, res_out, coef_out,
-    r, w, sol, cn, un, fin, in_sems, out_sems,
+    fields, panels, fin, in_sems, out_sems,
 ):
-    cols, dofs = r.shape
-    recy = cn.shape[0]
+    _, cols, dofs = fields.shape
+    recy = panels.shape[1]
     width = dofs // PARTS
-    coef_copy = pltpu.make_async_copy(coef_in, coef_out, out_sems.at[0, 0])
-    coef_copy.start()
     fin_copy = pltpu.make_async_copy(fin_in, fin, out_sems.at[0, 1])
     fin_copy.start()
     loads, outs = [], []
     for i in range(PARTS):
         span = pl.ds(i * width, width)
-        pairs = ((cn_in, cn), (w_in, w), (r_in, r), (un_in, un), (base_in, sol))
         loads.append(
             [
-                pltpu.make_async_copy(src.at[:, span], dst.at[:, span], in_sems.at[i, j])
-                for j, (src, dst) in enumerate(pairs)
+                pltpu.make_async_copy(src.at[:, :, span], dst.at[:, :, span], in_sems.at[i, j])
+                for j, (src, dst) in enumerate(((panels_in, panels), (fields_in, fields)))
             ]
         )
         for load in loads[-1]:
             load.start()
+    coef_copy = pltpu.make_async_copy(coef_in, coef_out, out_sems.at[0, 0])
+    coef_copy.start()
     fin_copy.wait()
     proj, step = fin[:, :recy], fin[:, recy : recy + 1]
     high = proj.astype(BF16)
@@ -544,13 +541,13 @@
         for load in loads[i]:
             load.wait()
         at = slice(i * width, (i + 1) * width)
-        old = r[:, at]
-        r[:, at] = old - step * (w[:, at] - halves(nn(proj2, cn[:, at])))
+        old = fields[0, :, at]
+        fields[0, :, at] = old - step * (fields[1, :, at] - halves(nn(proj2, panels[0, :, at])))
         rounded = old.astype(BF16).astype(F32)
-        sol[:, at] = sol[:, at] + step * (rounded - halves(nn(proj2, un[:, at])))
-        for j, (src, dst) in enumerate(((r, res_out), (sol, sol_out))):
+        fields[2, :, at] = fields[2, :, at] + step * (rounded - halves(nn(proj2, panels[1, :, at])))
+        for j, dst in ((0, res_out), (2, sol_out)):
             span = pl.ds(i * width, width)
-            out = pltpu.make_async_copy(src.at[:, span], dst.at[:, span], out_sems.at[i + 1, j])
+            out = pltpu.make_async_copy(fields.at[j, :, span], dst.at[:, span], out_sems.at[i + 1, j // 2])
             out.start()
             outs.append(out)
     coef_copy.wait()
@@ -572,16 +569,13 @@
     middle = pl.pallas_call(
         functools.partial(kernel, n_mesh, n_samp),
         out_shape=(
-            jax.ShapeDtypeStruct((cols, dofs), F32),
-            jax.ShapeDtypeStruct((cols, dofs), F32),
-            jax.ShapeDtypeStruct((cols, dofs), F32),
-            jax.ShapeDtypeStruct((recy, dofs), BF16),
-            jax.ShapeDtypeStruct((recy, dofs), BF16),
+            jax.ShapeDtypeStruct((3, cols, dofs), F32),
+            jax.ShapeDtypeStruct((2, recy, dofs), BF16),
             jax.ShapeDtypeStruct((cols, LANES), F32),
             jax.ShapeDtypeStruct((recy, cols), F32),
         ),
         in_specs=[hbm] * 8,
-        out_specs=(hbm,) * 7,
+        out_specs=(hbm,) * 4,
         scratch_shapes=[
             field,
             field,
@@ -642,7 +636,6 @@
         send_list,
         part_sizes,
     )
-    plain = pltpu.VMEM((recy, dofs), BF16)
     return pl.pallas_call(
         last_kernel,
         out_shape=(
@@ -650,16 +643,13 @@
             jax.ShapeDtypeStruct((cols, dofs), F32),
             jax.ShapeDtypeStruct((recy, cols), F32),
         ),
-        in_specs=[hbm] * 7,
+        in_specs=[hbm] * 4,
         out_specs=(hbm,) * 3,
         scratch_shapes=[
-            field,
-            field,
-            field,
-            plain,
-            plain,
+            pltpu.VMEM((3, cols, dofs), F32),
+            pltpu.VMEM((2, recy, dofs), BF16),
             pltpu.VMEM((cols, LANES), F32),
-            dma((PARTS, 5)),
+            dma((PARTS, 2)),
             dma((PARTS + 1, 2)),
         ],
         compiler_params=pltpu.CompilerParams(vmem_limit_bytes=62 << 20),

time: 68.7 us -> 68.2 us (level)
  no operation moved by 1% of the time
where the time goes in v5:
time: 68.2 us; the launch traced here: 68.1 us
  Pallas kernels  66.8 us (98%)
  between operations  1.29 us (2%)
    pallas_call x1, Pallas kernels, per_device(): pl.pallas_call(functools.partial(kernel, n_mesh, n_samp), out_shape=(jax....  63.6 us
    pallas_call x1, Pallas kernels, per_device(): pl.pallas_call(last_kernel, out_shape=(jax.ShapeDtypeStruct((cols, dofs),...  3.2 us

profile of v5, /device:TPU:1, one launch (start us, length us, event | category | flops | bytes accessed | tf_op | source)
XLA Modules:
  0.0 68.1 jit_solution(3202125710074511899)
XLA Ops:
  1.3 63.6 %shard_map.103 = (f32[3,64,3072]{2,1,0:T(8,128)}, bf16[2,64,3072]{2,1,0:T(8,128)(2,1)}, f32[64,128]{1,0:T(8,128)}, f32[64,64]{1,0:T(8,128)}) custom-call(f32[64,3072]{1,0:T(8,128)} %resid.1, bf16[4,3072]{1,0:T(4,128)(2,1)} %u_in.1, bf16[4,3072]{1,0:T(4,128)(2,1)} %c_in.1, bf16[3072,1152]{1,0:T(8,128)(2,1)} %bitcast.3, f32[1,3072]{1,0:T(1,128)} %bitcast.4, ...), custom_call_target="tpu_custom_call" | custom-call | tf_op jit(solution)/shard_map/pallas_call | solution.py:569
  64.9 3.2 %shard_map.104 = (f32[64,3072]{1,0:T(8,128)}, f32[64,3072]{1,0:T(8,128)}, f32[64,64]{1,0:T(8,128)}) custom-call(f32[3,64,3072]{2,1,0:T(8,128)} %get-tuple-element.7.fields_in, bf16[2,64,3072]{2,1,0:T(8,128)(2,1)} %get-tuple-element.8.panels_in, f32[64,128]{1,0:T(8,128)} %get-tuple-element.9.fin_in, f32[64,64]{1,0:T(8,128)} %get-tuple-element.10.coef_in), custom_call_target="tpu_custom_call" | custom-call | tf_op jit(solution)/shard_map/pallas_call | solution.py:639

commit v6 on v5

--- a/solution.py
+++ b/solution.py
@@ -64,7 +64,6 @@
     wide = dofs // quarters // LANES
     pairs = dofs // PAIR
     low_half = lax.broadcasted_iota(jnp.int32, (cols, LANES), 1) < LANES // 2
-    highest = lax.Precision.HIGHEST
 
     loads = [
         pltpu.make_async_copy(src, dst, in_sems.at[i])
@@ -148,19 +147,32 @@
                 out[recy:, at : at + LANES] = tile
 
     span = chips // 2
+    back = span // 2 - 1
     part = lax.rem(chip, span)
     reducer = core == lax.rem(part, 2)
     own_sum = lax.div(chip, span) * TILES + part
     all_sums = 2 * TILES
 
-    def rs_send(which, value):
+    rows_packed = cols // 2 // TILES
+    eye = lax.broadcasted_iota(jnp.int32, (cols, cols), 0) == lax.broadcasted_iota(jnp.int32, (cols, cols), 1)
+
+    def as_row(column):
+        return jnp.sum(jnp.where(eye, column, 0.0), axis=0, keepdims=True)
+
+    def as_column(row):
+        return jnp.sum(jnp.where(eye, row, 0.0), axis=1, keepdims=True)
+
+    def rs_send(which, value, extra):
+        packed = jnp.concatenate([value[: cols // 2], value[cols // 2 :]], 1)
         for t in range(TILES):
-            pay[which, t] = value[8 * t : 8 * t + 8, :]
-
-        def one(t, carry):
-            away = lax.rem(chip - t + chips + span // 2 - 1, chips)
-            slot = 2 * lax.rem(away, span) + core
-            target = 2 * lax.rem(t + span * lax.div(away, span), chips) + lax.rem(t, 2)
+            pay[which, t, :rows_packed] = packed[rows_packed * t : rows_packed * (t + 1), :]
+            pay[which, t, rows_packed:] = extra
+
+        for ahead in sorted(range(span), key=lambda k: -abs(k - back)):
+            t = lax.rem(chip + back - ahead + chips, span)
+            slot = 2 * ahead + core
+            near = lax.rem(chip + back - ahead + chips, chips)
+            target = 2 * near + lax.rem(t, 2)
 
             @pl.when(target != me)
             def _():
@@ -177,10 +189,6 @@
             def _():
                 rs_got[which, slot] = pay[which, t]
 
-            return carry
-
-        lax.fori_loop(0, TILES, one, 0)
-
     def tiles_done(sem, count):
         some = ar_got.at[pl.ds(0, count)]
         pltpu.make_async_copy(some, some, sem).wait()
@@ -195,9 +203,8 @@
             at = which * all_sums + own_sum
             ar_got[at] = total
 
-            def one(o, carry):
-                half = lax.div(o + 1, 2)
-                ahead = n_mesh // 2 + half * (1 - 2 * lax.rem(o, 2))
+            half = n_mesh // 2
+            for ahead in sorted(range(1, n_mesh), key=lambda k: abs(k - half)):
                 pltpu.make_async_remote_copy(
                     src_ref=ar_got.at[at],
                     dst_ref=ar_got.at[at],
@@ -206,9 +213,6 @@
                     device_id={"mesh": lax.rem(me + ahead, n_mesh)},
                     device_id_type=MESH,
                 ).start()
-                return carry
-
-            lax.fori_loop(0, n_mesh - 1, one, 0)
 
     def ar_wait(which):
         @pl.when(reducer)
@@ -220,7 +224,10 @@
             tiles_done(ag_rsem.at[which], all_sums)
 
         at = which * all_sums
-        return jnp.concatenate([ar_got[at + t] + ar_got[at + TILES + t] for t in range(TILES)], 0)
+        tiles = [ar_got[at + t] + ar_got[at + TILES + t] for t in range(TILES)]
+        packed = jnp.concatenate([tile[:rows_packed] for tile in tiles], 0)
+        value = jnp.concatenate([packed[:, :recy], packed[:, recy:]], 0)
+        return value, tiles[0][rows_packed:]
 
     def ar_sent(which):
         @pl.when(reducer)
@@ -379,14 +386,18 @@
         proj = halves(nt(wb[...], cn[:recy]))
         ww = jnp.sum(ww, axis=1, keepdims=True)
         wr = jnp.sum(wr, axis=1, keepdims=True)
-        lane = lax.broadcasted_iota(jnp.int32, (cols, LANES - recy), 1)
-        return jnp.concatenate([proj, jnp.where(lane == 0, ww, jnp.where(lane == 1, wr, 0.0))], 1)
+        return proj, jnp.concatenate([as_row(ww), as_row(wr)], 1)
+
+    def times_gram(x):
+        high = x.astype(BF16).astype(F32)
+        gram_high = gram.astype(BF16).astype(F32)
+        left = jnp.concatenate([high, x - high, high], 1).astype(BF16)
+        return nn(left, jnp.concatenate([gram_high, gram_high, gram - gram_high], 0).astype(BF16))
 
     def step_of(reduced, c_r):
-        proj = reduced[:, :recy]
-        ww = reduced[:, recy : recy + 1]
-        wr = reduced[:, recy + 1 : recy + 2]
-        p_gram = jnp.dot(proj, gram, precision=highest, preferred_element_type=F32)
+        proj, extra = reduced
+        ww, wr = as_column(extra[:, :cols]), as_column(extra[:, cols:])
+        p_gram = times_gram(proj)
         bottom = ww + jnp.sum(proj * (p_gram - 2.0 * proj), axis=1, keepdims=True)
         top = wr - jnp.sum(proj * c_r, axis=1, keepdims=True)
         step = top / bottom
@@ -419,9 +430,10 @@
     wait_panel(0, panel_rsem)
     natural(0, cn)
     first = nt(jnp.concatenate([rb[...], cn[:recy]], 0), cn[:recy])
-    rs_send(0, jnp.concatenate([first[:cols], first[cols:]], 1))
-
-    send_panel(1)
+    no_extra = jnp.zeros((1, LANES), F32)
+    rs_send(0, first[:cols], no_extra)
+    rs_send(ITERS + 1, first[cols:], no_extra)
+
     def fill_panel(m, carry):
         at = pl.multiple_of(m * PAIR, PAIR)
         fill_tables(m, 2 * cols, [cn[:recy, pl.ds(at + j * LANES, LANES)].astype(F32) for j in range(3)])
@@ -441,29 +453,28 @@
         copy.wait()
     take_ghosts(got_c, 2 * cols, recy)
     apply_stiff(2 * cols + recy, emit_first)
-    reduced = ar_wait(0)
-    coef = reduced[:, :recy]
-    gram = reduced[:, recy:]
+    coef, _ = ar_wait(0)
     coef2 = split2(coef)
 
     def make_first(span):
         new_r = r[:, span] - nn(coef2, cn[:, span])
         return new_r, a[:, span] - nn(coef2, dn[:, span])
 
-    rs_send(1, renew(make_first, r, a))
+    rs_send(1, *renew(make_first, r, a))
 
     coef_t[...] = coef.T
-    c_r = coef - jnp.dot(coef, gram, precision=highest, preferred_element_type=F32)
     fill_split(a)
     pack_ghosts(send_f.at[1], 0, 2 * cols, ghost_copies(send_f.at[1], got_f.at[1], 2))
+    ag_send(ITERS + 1)
     apply_own(2 * cols)
-    wait_panel(1, panel_rsem)
-    natural(1, un)
     ag_send(1)
+    send_panel(1)
     for copy in ghost_copies(send_f.at[1], got_f.at[1], 2):
         copy.wait()
     take_ghosts(got_f.at[1], 0, 2 * cols)
     apply_stiff(2 * cols, emit_second)
+    gram, _ = ar_wait(ITERS + 1)
+    c_r = coef - times_gram(coef)
     proj, step1, c_r = step_of(ar_wait(1), c_r)
     proj2 = split2(proj)
 
@@ -472,8 +483,10 @@
         new_r = r[:, span] - step1 * (image - nn(proj2, cn[:, span]))
         return new_r, image - step1 * (b[:, span] - nn(proj2, dn[:, span]))
 
-    rs_send(2, renew(make_second, r_next, w_next))
-
+    rs_send(2, *renew(make_second, r_next, w_next))
+
+    wait_panel(1, panel_rsem)
+    natural(1, un)
     carried2 = split2(coef - step1 * proj)
 
     def base(m, carry):
@@ -502,6 +515,7 @@
     for which in range(2):
         wait_panel(which, panel_ssem)
         ar_sent(which)
+    ar_sent(ITERS + 1)
     ag_send(2)
     proj, step2, _ = step_of(ar_wait(2), c_r)
     fin[...] = jnp.concatenate([proj, jnp.broadcast_to(step2, (cols, LANES - recy))], 1)
@@ -561,6 +575,7 @@
     recy = recycle_c.shape[0] * n_samp
     wide = dofs * recycle_c.shape[0] // 16 // LANES
     ext = blocks + 2 * GHOST
+    tile = cols // 2 // TILES + 1
     hbm = pl.BlockSpec(memory_space=pltpu.HBM)
     dma = pltpu.SemaphoreType.DMA
     field = pltpu.VMEM((cols, dofs), F32)
@@ -608,18 +623,18 @@
             pltpu.VMEM((ITERS, 2, GHOST + GHOST // 2, 2 * cols, LANES), BF16),
             pltpu.VMEM((2, GHOST + GHOST // 2, recy, LANES), BF16),
             pltpu.VMEM((2, GHOST + GHOST // 2, recy, LANES), BF16),
-            pltpu.VMEM((ITERS + 1, TILES, 8, LANES), F32),
-            pltpu.VMEM((ITERS + 1, n_mesh // 2, 8, LANES), F32),
-            pltpu.VMEM(((ITERS + 1) * 2 * TILES, 8, LANES), F32),
+            pltpu.VMEM((ITERS + 2, TILES, tile, LANES), F32),
+            pltpu.VMEM((ITERS + 2, n_mesh // 2, tile, LANES), F32),
+            pltpu.VMEM(((ITERS + 2) * 2 * TILES, tile, LANES), F32),
             dma((8,)),
             dma((2,)),
             dma((2,)),
             dma((ITERS + 1, 2)),
             dma((ITERS + 1, 2)),
-            dma((ITERS + 1,)),
-            dma((ITERS + 1,)),
-            dma((ITERS + 1,)),
-            dma((ITERS + 1,)),
+            dma((ITERS + 2,)),
+            dma((ITERS + 2,)),
+            dma((ITERS + 2,)),
+            dma((ITERS + 2,)),
             dma((7,)),
             pltpu.SemaphoreType.REGULAR,
         ],

time: 68.2 us -> 67.9 us (level)
  no operation moved by 1% of the time
where the time goes in v6:
time: 67.9 us; the launch traced here: 67.8 us
  Pallas kernels  66.5 us (98%)
  between operations  1.29 us (2%)
    pallas_call x1, Pallas kernels, per_device(): pl.pallas_call(functools.partial(kernel, n_mesh, n_samp), out_shape=(jax....  63.3 us
    pallas_call x1, Pallas kernels, per_device(): pl.pallas_call(last_kernel, out_shape=(jax.ShapeDtypeStruct((cols, dofs),...  3.2 us

profile of v6, /device:TPU:1, one launch (start us, length us, event | category | flops | bytes accessed | tf_op | source)
XLA Modules:
  0.0 67.8 jit_solution(5081686260815103014)
XLA Ops:
  1.3 63.3 %shard_map.103 = (f32[3,64,3072]{2,1,0:T(8,128)}, bf16[2,64,3072]{2,1,0:T(8,128)(2,1)}, f32[64,128]{1,0:T(8,128)}, f32[64,64]{1,0:T(8,128)}) custom-call(f32[64,3072]{1,0:T(8,128)} %resid.1, bf16[4,3072]{1,0:T(4,128)(2,1)} %u_in.1, bf16[4,3072]{1,0:T(4,128)(2,1)} %c_in.1, bf16[3072,1152]{1,0:T(8,128)(2,1)} %bitcast.3, f32[1,3072]{1,0:T(1,128)} %bitcast.4, ...), custom_call_target="tpu_custom_call" | custom-call | tf_op jit(solution)/shard_map/pallas_call | solution.py:584
  64.6 3.2 %shard_map.104 = (f32[64,3072]{1,0:T(8,128)}, f32[64,3072]{1,0:T(8,128)}, f32[64,64]{1,0:T(8,128)}) custom-call(f32[3,64,3072]{2,1,0:T(8,128)} %get-tuple-element.7.fields_in, bf16[2,64,3072]{2,1,0:T(8,128)(2,1)} %get-tuple-element.8.panels_in, f32[64,128]{1,0:T(8,128)} %get-tuple-element.9.fin_in, f32[64,64]{1,0:T(8,128)} %get-tuple-element.10.coef_in), custom_call_target="tpu_custom_call" | custom-call | tf_op jit(solution)/shard_map/pallas_call | solution.py:654

commit v7 on v6

--- a/solution.py
+++ b/solution.py
@@ -16,7 +16,7 @@
 SLOTS = 6
 GHOST = 8
 ITERS = 2
-TILES = 8
+TILES = 4
 REACH = 4
 SQUARE = 4
 PARTS = 2
@@ -149,7 +149,7 @@
     span = chips // 2
     back = span // 2 - 1
     part = lax.rem(chip, span)
-    reducer = core == lax.rem(part, 2)
+    reducer = jnp.logical_and(core == lax.rem(part, 2), part < TILES)
     own_sum = lax.div(chip, span) * TILES + part
     all_sums = 2 * TILES
 
@@ -168,14 +168,13 @@
             pay[which, t, :rows_packed] = packed[rows_packed * t : rows_packed * (t + 1), :]
             pay[which, t, rows_packed:] = extra
 
-        for ahead in sorted(range(span), key=lambda k: -abs(k - back)):
-            t = lax.rem(chip + back - ahead + chips, span)
-            slot = 2 * ahead + core
-            near = lax.rem(chip + back - ahead + chips, chips)
-            target = 2 * near + lax.rem(t, 2)
+        for t in range(TILES):
+            away = lax.rem(chip - t + chips + back, chips)
+            slot = 2 * lax.rem(away, span) + core
+            target = 2 * lax.rem(t + span * lax.div(away, span), chips) + t % 2
 
             @pl.when(target != me)
-            def _():
+            def _(t=t, slot=slot, target=target):
                 pltpu.make_async_remote_copy(
                     src_ref=pay.at[which, t],
                     dst_ref=rs_got.at[which, slot],
@@ -186,7 +185,7 @@
                 ).start()
 
             @pl.when(target == me)
-            def _():
+            def _(t=t, slot=slot):
                 rs_got[which, slot] = pay[which, t]
 
     def tiles_done(sem, count):

time: 67.9 us -> 69.2 us (1.019)
  Pallas kernels: 66.5 us -> 67.8 us
    pallas_call x1, Pallas kernels: 63.3 us -> 64.6 us  [per_device(): pl.pallas_call(functools.partial(kernel, n_mesh, n_samp), out_shape=(jax....]
where the time goes in v7:
time: 69.2 us; the launch traced here: 69.1 us
  Pallas kernels  67.8 us (98%)
  between operations  1.29 us (2%)
    pallas_call x1, Pallas kernels, per_device(): pl.pallas_call(functools.partial(kernel, n_mesh, n_samp), out_shape=(jax....  64.6 us
    pallas_call x1, Pallas kernels, per_device(): pl.pallas_call(last_kernel, out_shape=(jax.ShapeDtypeStruct((cols, dofs),...  3.2 us

profile of v7, /device:TPU:1, one launch (start us, length us, event | category | flops | bytes accessed | tf_op | source)
XLA Modules:
  0.0 69.1 jit_solution(8680663745637267349)
XLA Ops:
  1.3 64.6 %shard_map.103 = (f32[3,64,3072]{2,1,0:T(8,128)}, bf16[2,64,3072]{2,1,0:T(8,128)(2,1)}, f32[64,128]{1,0:T(8,128)}, f32[64,64]{1,0:T(8,128)}) custom-call(f32[64,3072]{1,0:T(8,128)} %resid.1, bf16[4,3072]{1,0:T(4,128)(2,1)} %u_in.1, bf16[4,3072]{1,0:T(4,128)(2,1)} %c_in.1, bf16[3072,1152]{1,0:T(8,128)(2,1)} %bitcast.3, f32[1,3072]{1,0:T(1,128)} %bitcast.4, ...), custom_call_target="tpu_custom_call" | custom-call | tf_op jit(solution)/shard_map/pallas_call | solution.py:583
  65.9 3.2 %shard_map.104 = (f32[64,3072]{1,0:T(8,128)}, f32[64,3072]{1,0:T(8,128)}, f32[64,64]{1,0:T(8,128)}) custom-call(f32[3,64,3072]{2,1,0:T(8,128)} %get-tuple-element.7.fields_in, bf16[2,64,3072]{2,1,0:T(8,128)(2,1)} %get-tuple-element.8.panels_in, f32[64,128]{1,0:T(8,128)} %get-tuple-element.9.fin_in, f32[64,64]{1,0:T(8,128)} %get-tuple-element.10.coef_in), custom_call_target="tpu_custom_call" | custom-call | tf_op jit(solution)/shard_map/pallas_call | solution.py:653
